TPU v7x, 32 devices: a whole 2x2x4 slice. The times are simulated.
32 devices in a mesh: tm: 16 (over z, y, core), rows: 2 (over x).
Axes of the slice: x: 2, y: 2, z: 4, core: 2. Of those that a mesh axis runs over, the one named last changes fastest.
Arguments:
- noisy_states: float32 [64, 2, 16, 256], P('tm', None, 'rows'), may hold values from -6 to 6
- noise_first: float32 [64, 2, 16, 256], P('tm', None, 'rows'), may hold values from -6 to 6
- noise_second: float32 [64, 2, 16, 256], P('tm', None, 'rows'), may hold values from -6 to 6
- conv_in: bfloat16 [9, 96, 18], replicated, may hold values from -0.5 to 0.5
- conv_out: bfloat16 [9, 2, 96], replicated, may hold values from -0.21875 to 0.21875
- level_embed: float32 [96], replicated, may hold values from -4 to 4
- obs_count: int32 [16, 2], P('tm', 'rows'), may hold values from 1 to 256, as said below
- obs_step: int32 [16, 2, 256], P('tm', 'rows'), may hold values from 0 to 3
- obs_row: int32 [16, 2, 256], P('tm', 'rows'), may hold values from 0 to 7
- obs_col: int32 [16, 2, 256], P('tm', 'rows'), may hold values from 0 to 255
- obs_value: float32 [16, 2, 256], P('tm', 'rows'), may hold values from -4 to 4
Outputs:
- final_states: float32 [64, 2, 16, 256], P('tm', None, 'rows')
Inputs may be any that keep to these rules, and one draw needn't show every extreme that they name: `obs_count`: some block has exactly 256 live observations in every draw; the counts are skewed over blocks.
All inputs are finite; a program needn't handle non-finite values.
Results may differ from a plain program's by a relative error of at most 0.0014.
Values may be sent and summed in bfloat16 or wider, within the bound.
No kernel may reach another device: no remote copies, remote signals or barrier semaphores. Data moves between devices by JAX's collectives and lax.ppermute only.
A program may use at most 64 MiB of HBM per device.

v0:
```python
import jax
import jax.numpy as jnp
from jax import lax
from jax.sharding import PartitionSpec as P

K = 4


LEVELS = (1.0, 0.5, 0.2)
OBS_NOISE = 0.1
COVARIANCE_GAIN = 0.5


def with_halo(cells, sides, width, closed):
    for axis, dim in sides:
        count = lax.axis_size(axis)
        ends = count if closed else count - 1
        head = lax.slice_in_dim(cells, 0, width, axis=dim)
        tail = lax.slice_in_dim(cells, cells.shape[dim] - width, cells.shape[dim], axis=dim)
        cells = jnp.concatenate(
            [
                lax.ppermute(tail, axis, [(i, (i + 1) % count) for i in range(ends)]),
                cells,
                lax.ppermute(head, axis, [((i + 1) % count, i) for i in range(ends)]),
            ],
            axis=dim,
        )
    return cells


def conv_three(window, weights, out_rows):
    summed = jnp.zeros((weights.shape[1], out_rows, window.shape[2]), jnp.float32)
    for row_off in range(3):
        for col_off in range(3):
            shifted = jnp.roll(window[:, row_off : row_off + out_rows, :], 1 - col_off, axis=2)
            summed = summed + jnp.einsum(
                "oc,crw->orw",
                weights[3 * row_off + col_off],
                shifted,
                preferred_element_type=jnp.float32,
            )
    return summed


def denoise_net(scaled, conv_in, conv_out, level_embed, level_now):
    frames_here, layer_count, rows_here, columns = scaled.shape
    rim_width = 2
    framed = with_halo(scaled, (("tm", 0),), K, False)
    padded = with_halo(framed, (("rows", 2),), rim_width, True)
    hidden_rows = rows_here + 2 * (rim_width - 1)
    channels = layer_count * (2 * K + 1)

    def hidden_at(position):
        window = lax.dynamic_slice_in_dim(padded, position, 2 * K + 1, 0).reshape(
            channels, rows_here + 2 * rim_width, columns
        )
        summed = conv_three(window, conv_in, hidden_rows) + level_now * level_embed[:, None, None]
        return jax.nn.silu(summed).astype(jnp.bfloat16)

    hidden = lax.map(hidden_at, jnp.arange(frames_here, dtype=jnp.int32))

    def output_at(block):
        return conv_three(block, conv_out, rows_here)

    return lax.map(output_at, hidden)


def observe_guide(denoised, level_now, live_count, cell_index, col_index, values):
    frames_here, layer_count, rows_here, columns = denoised.shape
    upper = denoised[:, 0].reshape(frames_here * rows_here, columns)
    slots = cell_index.shape[0]
    active_slot = jnp.arange(slots, dtype=jnp.int32) < live_count
    cells_hot = (
        cell_index[:, None] == jnp.arange(frames_here * rows_here, dtype=jnp.int32)[None, :]
    ).astype(jnp.float32)
    cols_hot = (col_index[:, None] == jnp.arange(columns, dtype=jnp.int32)[None, :]).astype(
        jnp.float32
    )
    picked = jnp.sum(jnp.dot(cells_hot, upper, precision=lax.Precision.HIGHEST) * cols_hot, axis=1)
    misfit = jnp.where(
        active_slot,
        (values - picked) / (OBS_NOISE + COVARIANCE_GAIN * level_now**2),
        jnp.float32(0.0),
    )
    guide_upper = jnp.dot(cells_hot.T, cols_hot * misfit[:, None], precision=lax.Precision.HIGHEST)
    guide_upper = guide_upper.reshape(frames_here, 1, rows_here, columns)
    lower_zero = jnp.zeros((frames_here, layer_count - 1, rows_here, columns), jnp.float32)
    return jnp.concatenate([guide_upper, lower_zero], axis=1)


def per_device(
    noisy_states,
    noise_first,
    noise_second,
    conv_in,
    conv_out,
    level_embed,
    obs_count,
    obs_step,
    obs_row,
    obs_col,
    obs_value,
):
    rows_here = noisy_states.shape[2]
    live_count = obs_count.reshape(-1)[0]
    cell_index = obs_step.reshape(-1) * rows_here + obs_row.reshape(-1)
    col_index = obs_col.reshape(-1)
    values = obs_value.reshape(-1)
    current = noisy_states
    for index_level, noise_draw in enumerate((noise_first, noise_second)):
        level_now = LEVELS[index_level]
        level_next = LEVELS[index_level + 1]
        scaled = (current / jnp.sqrt(1.0 + level_now**2)).astype(jnp.bfloat16)
        net = denoise_net(scaled, conv_in, conv_out, level_embed, level_now)
        denoised = current / (1.0 + level_now**2) + level_now / jnp.sqrt(1.0 + level_now**2) * net
        guide = observe_guide(denoised, level_now, live_count, cell_index, col_index, values)
        score = (denoised - current) / level_now**2 + guide
        spread = level_now**2 - level_next**2
        current = current + spread * score + spread**0.5 * noise_draw
    return current


def solution(mesh):
    in_specs = (
        P("tm", None, "rows", None),
        P("tm", None, "rows", None),
        P("tm", None, "rows", None),
        P(),
        P(),
        P(),
        P("tm", "rows"),
        P("tm", "rows", None),
        P("tm", "rows", None),
        P("tm", "rows", None),
        P("tm", "rows", None),
    )
    out_specs = P("tm", None, "rows", None)
    return jax.shard_map(
        per_device, mesh=mesh, in_specs=in_specs, out_specs=out_specs, check_vma=False
    )
```

profile of v0, /device:TPU:15, one launch (start us, length us, event | category | flops | bytes accessed | tf_op | source)
XLA Modules:
  0.0 105.9 jit_solution(7429263584404429213)
XLA Ops:
  0.0 0.9 multiply_convert_fusion.3
  0.9 3.7 %collective-permute-start = (bf16[4,2,8,256]{3,2,1,0:T(8,128)(2,1)S(1)}, bf16[4,2,8,256]{3,2,1,0:T(8,128)(2,1)S(1)}, u32[]{:S(2)}, u32[]{:S(2)}) collective-permute-start(bf16[4,2,8,256]{3,2,1,0:T(8,128)(2,1)S(1)} %multiply_convert_fusion.3), channel_id=1, source_target_pairs={{0,2},{2,4},{4,6},{6,8},{8,10},{10,12},{12,14},{14,16},{16,18},{18... | collective-permute-start | bytes 98312 | tf_op jit(solution)/shard_map/ppermute | solution.py:22
  4.6 1.9 %collective-permute-start.1 = (bf16[4,2,8,256]{3,2,1,0:T(8,128)(2,1)S(1)}, bf16[4,2,8,256]{3,2,1,0:T(8,128)(2,1)S(1)}, u32[]{:S(2)}, u32[]{:S(2)}) collective-permute-start(bf16[4,2,8,256]{3,2,1,0:T(8,128)(2,1)S(1)} %multiply_convert_fusion.3), channel_id=1, source_target_pairs={{2,0},{4,2},{6,4},{8,6},{10,8},{12,10},{14,12},{16,14},{18,16},{20... | collective-permute-start | bytes 98312 | tf_op jit(solution)/shard_map/ppermute | solution.py:24
  6.5 4.2 %collective-permute-done.1 = bf16[4,2,8,256]{3,2,1,0:T(8,128)(2,1)S(1)} collective-permute-done((bf16[4,2,8,256]{3,2,1,0:T(8,128)(2,1)S(1)}, bf16[4,2,8,256]{3,2,1,0:T(8,128)(2,1)S(1)}, u32[]{:S(2)}, u32[]{:S(2)}) %collective-permute-start.1) | collective-permute-done | bytes 32800 | tf_op jit(solution)/shard_map/ppermute | solution.py:24
  11.1 1.2 %collective-permute-start.3 = (bf16[12,2,2,256]{3,2,1,0:T(2,128)(2,1)S(1)}, bf16[12,2,2,256]{3,2,1,0:T(2,128)(2,1)S(1)}, u32[]{:S(2)}, u32[]{:S(2)}) collective-permute-start(bf16[12,2,2,256]{3,2,1,0:T(2,128)(2,1)S(1)} %get-tuple-element.234), channel_id=1, source_target_pairs={{1,0},{0,1},{3,2},{2,3},{5,4},{4,5},{7,6},{6,7},{9,8},{8,9},{11,10... | collective-permute-start | bytes 73736 | tf_op jit(solution)/shard_map/ppermute | solution.py:24
  12.3 0.7 multiply_add_fusion.4
  14.2 26.1 %while.40 = (s32[]{:T(128)}, bf16[4,96,10,256]{3,1,2,0:T(8,128)(2,1)S(1)}, s32[4]{0:T(128)S(1)}, bf16[12,2,12,256]{3,1,0,2:T(2,128)(2,1)S(1)}, bf16[9,96,18]{1,2...) while((s32[]{:T(128)}, bf16[4,96,10,256]{3,1,2,0:T(8,128)(2,1)S(1)}, ...), condition=%wide.region_1.2_spmd, body=%wide.region_0.1_spmd.sunk | while | flops 84172800 | bytes 19372692 | solution.py:60
  14.3 0.7 dynamic_slice.31
  19.5 0.4 fusion.401
  20.3 0.5 fusion.402
  20.8 0.7 dynamic_slice.31
  25.0 0.4 fusion.400
  26.8 0.5 fusion.402
  27.3 0.7 dynamic_slice.31
  33.3 0.5 fusion.402
  33.8 0.7 dynamic_slice.31
  39.8 0.5 fusion.402
  40.4 12.3 %while.41 = (s32[]{:T(128)}, f32[4,2,8,256]{3,2,1,0:T(8,128)S(1)}, bf16[4,96,10,256]{3,1,2,0:T(8,128)(2,1)S(1)}, bf16[9,2,96]{2,1,0:T(2,128)(2,1)S(1)}, s32[]{:T(128)}) while((s32[]{:T(128)}, f32[4,2,8,256]{3,2,1,0:T(8,128)S(1)}, bf16[4,96,10,256]{3,1,2,0:T(8,128)(2,1)S(1)}, bf16[9,2,96]{2,1,0:T(2,128)(2,1)S(1)}, s32[]{:T(128)}) %tuple.134), condition=%wide.region_3.4_spmd, body=%wide.region_2.3_spmd.sunk | while | flops 11829250 | bytes 11031109 | solution.py:65
  40.5 0.5 fusion.422
  43.6 0.5 fusion.422
  46.6 0.5 fusion.422
  49.7 0.5 fusion.422
  52.8 0.4 fusion.222
  53.6 3.3 %collective-permute-start.4 = (bf16[4,2,8,256]{3,2,1,0:T(8,128)(2,1)S(1)}, bf16[4,2,8,256]{3,2,1,0:T(8,128)(2,1)S(1)}, u32[]{:S(2)}, u32[]{:S(2)}) collective-permute-start(bf16[4,2,8,256]{3,2,1,0:T(8,128)(2,1)S(1)} %get-tuple-element.181), channel_id=1, source_target_pairs={{0,2},{2,4},{4,6},{6,8},{8,10},{10,12},{12,14},{14,16},{16,18},{18... | collective-permute-start | bytes 98312 | tf_op jit(solution)/shard_map/ppermute | solution.py:22
  57.0 2.1 %collective-permute-start.5 = (bf16[4,2,8,256]{3,2,1,0:T(8,128)(2,1)S(1)}, bf16[4,2,8,256]{3,2,1,0:T(8,128)(2,1)S(1)}, u32[]{:S(2)}, u32[]{:S(2)}) collective-permute-start(bf16[4,2,8,256]{3,2,1,0:T(8,128)(2,1)S(1)} %get-tuple-element.181), channel_id=1, source_target_pairs={{2,0},{4,2},{6,4},{8,6},{10,8},{12,10},{14,12},{16,14},{18,16},{20... | collective-permute-start | bytes 98312 | tf_op jit(solution)/shard_map/ppermute | solution.py:24
  59.1 4.0 %collective-permute-done.5 = bf16[4,2,8,256]{3,2,1,0:T(8,128)(2,1)S(1)} collective-permute-done((bf16[4,2,8,256]{3,2,1,0:T(8,128)(2,1)S(1)}, bf16[4,2,8,256]{3,2,1,0:T(8,128)(2,1)S(1)}, u32[]{:S(2)}, u32[]{:S(2)}) %collective-permute-start.5) | collective-permute-done | bytes 32800 | tf_op jit(solution)/shard_map/ppermute | solution.py:24
  63.2 1.3 %collective-permute-start.6 = (bf16[12,2,2,256]{3,2,1,0:T(2,128)(2,1)S(1)}, bf16[12,2,2,256]{3,2,1,0:T(2,128)(2,1)S(1)}, u32[]{:S(2)}, u32[]{:S(2)}) collective-permute-start(bf16[12,2,2,256]{3,2,1,0:T(2,128)(2,1)S(1)} %get-tuple-element.231), channel_id=1, source_target_pairs={{0,1},{1,0},{2,3},{3,2},{4,5},{5,4},{6,7},{7,6},{8,9},{9,8},{10,11... | collective-permute-start | bytes 73736 | tf_op jit(solution)/shard_map/ppermute | solution.py:22
  64.7 1.2 %collective-permute-done.6 = bf16[12,2,2,256]{3,2,1,0:T(2,128)(2,1)S(1)} collective-permute-done((bf16[12,2,2,256]{3,2,1,0:T(2,128)(2,1)S(1)}, bf16[12,2,2,256]{3,2,1,0:T(2,128)(2,1)S(1)}, u32[]{:S(2)}, u32[]{:S(2)}) %collective-permute-start.6) | collective-permute-done | bytes 24608 | tf_op jit(solution)/shard_map/ppermute | solution.py:22
  65.9 1.2 %collective-permute-done.7 = bf16[12,2,2,256]{3,2,1,0:T(2,128)(2,1)S(1)} collective-permute-done((bf16[12,2,2,256]{3,2,1,0:T(2,128)(2,1)S(1)}, bf16[12,2,2,256]{3,2,1,0:T(2,128)(2,1)S(1)}, u32[]{:S(2)}, u32[]{:S(2)}) %collective-permute-start.7) | collective-permute-done | bytes 24608 | tf_op jit(solution)/shard_map/ppermute | solution.py:24
  67.6 24.4 %while.42 = (s32[]{:T(128)}, bf16[4,96,10,256]{3,1,2,0:T(8,128)(2,1)S(1)}, s32[4]{0:T(128)S(1)}, bf16[12,2,12,256]{3,1,0,2:T(2,128)(2,1)S(1)}, bf16[9,96,18]{1,2...) while((s32[]{:T(128)}, bf16[4,96,10,256]{3,1,2,0:T(8,128)(2,1)S(1)}, ...), condition=%wide.region_6.7_spmd, body=%wide.region_5.6_spmd.sunk | while | flops 84172896 | bytes 19373460 | solution.py:60
  67.6 0.6 dynamic_slice.34
  73.2 0.5 fusion.460
  73.7 0.6 dynamic_slice.34
  79.3 0.5 fusion.460
  79.8 0.6 dynamic_slice.34
  84.7 0.4 fusion.459
  85.4 0.5 fusion.460
  85.9 0.6 dynamic_slice.34
  90.8 0.4 fusion.459
  91.5 0.5 fusion.460
  92.0 12.3 %while.43 = (s32[]{:T(128)}, f32[4,2,8,256]{3,2,1,0:T(8,128)S(1)}, bf16[4,96,10,256]{3,1,2,0:T(8,128)(2,1)S(1)}, bf16[9,2,96]{2,1,0:T(2,128)(2,1)S(1)}, s32[]{:T(128)}) while((s32[]{:T(128)}, f32[4,2,8,256]{3,2,1,0:T(8,128)S(1)}, bf16[4,96,10,256]{3,1,2,0:T(8,128)(2,1)S(1)}, bf16[9,2,96]{2,1,0:T(2,128)(2,1)S(1)}, s32[]{:T(128)}) %tuple.135), condition=%wide.region_8.9_spmd, body=%wide.region_7.8_spmd.sunk | while | flops 11829250 | bytes 11031109 | solution.py:65
  92.1 0.5 fusion.480
  95.2 0.5 fusion.480
  98.3 0.5 fusion.480
  101.3 0.5 fusion.480
  104.4 0.4 fusion.223
  104.8 0.4 convolution_bitcast_fusion
  105.2 0.7 multiply_add_fusion
  (232 shorter events, 46.3 us)
Async XLA Ops:
  0.0 14.2 %copy-start = (bf16[9,96,18]{1,2,0:T(8,128)(2,1)S(1)}, bf16[9,96,18]{1,2,0:T(8,128)(2,1)}, u32[]{:S(2)}) copy-start(bf16[9,96,18]{1,2,0:T(8,128)(2,1)} %param.22) | copy-start | bytes 93316
  0.0 14.2 %copy-start.7 = (f32[96]{0:T(128)S(1)}, f32[96]{0:T(128)}, u32[]{:S(2)}) copy-start(f32[96]{0:T(128)} %param.24) | copy-start | bytes 1156
  0.9 5.6 %collective-permute-start = (bf16[4,2,8,256]{3,2,1,0:T(8,128)(2,1)S(1)}, bf16[4,2,8,256]{3,2,1,0:T(8,128)(2,1)S(1)}, u32[]{:S(2)}, u32[]{:S(2)}) collective-permute-start(bf16[4,2,8,256]{3,2,1,0:T(8,128)(2,1)S(1)} %multiply_convert_fusion.3), channel_id=1, source_target_pairs={{0,2},{2,4},{4,6},{6,8},{8,10},{10,12},{12,14},{14,16},{16,18},{18... | collective-permute-start | bytes 98312 | tf_op jit(solution)/shard_map/ppermute | solution.py:22
  4.6 6.1 %collective-permute-start.1 = (bf16[4,2,8,256]{3,2,1,0:T(8,128)(2,1)S(1)}, bf16[4,2,8,256]{3,2,1,0:T(8,128)(2,1)S(1)}, u32[]{:S(2)}, u32[]{:S(2)}) collective-permute-start(bf16[4,2,8,256]{3,2,1,0:T(8,128)(2,1)S(1)} %multiply_convert_fusion.3), channel_id=1, source_target_pairs={{2,0},{4,2},{6,4},{8,6},{10,8},{12,10},{14,12},{16,14},{18,16},{20... | collective-permute-start | bytes 98312 | tf_op jit(solution)/shard_map/ppermute | solution.py:24
  10.7 2.9 %collective-permute-start.2 = (bf16[12,2,2,256]{3,2,1,0:T(2,128)(2,1)S(1)}, bf16[12,2,2,256]{3,2,1,0:T(2,128)(2,1)S(1)}, u32[]{:S(2)}, u32[]{:S(2)}) collective-permute-start(bf16[12,2,2,256]{3,2,1,0:T(2,128)(2,1)S(1)} %get-tuple-element.233), channel_id=1, source_target_pairs={{0,1},{1,0},{2,3},{3,2},{4,5},{5,4},{6,7},{7,6},{8,9},{9,8},{10,11... | collective-permute-start | bytes 73736 | tf_op jit(solution)/shard_map/ppermute | solution.py:22
  11.1 2.7 %collective-permute-start.3 = (bf16[12,2,2,256]{3,2,1,0:T(2,128)(2,1)S(1)}, bf16[12,2,2,256]{3,2,1,0:T(2,128)(2,1)S(1)}, u32[]{:S(2)}, u32[]{:S(2)}) collective-permute-start(bf16[12,2,2,256]{3,2,1,0:T(2,128)(2,1)S(1)} %get-tuple-element.234), channel_id=1, source_target_pairs={{1,0},{0,1},{3,2},{2,3},{5,4},{4,5},{7,6},{6,7},{9,8},{8,9},{11,10... | collective-permute-start | bytes 73736 | tf_op jit(solution)/shard_map/ppermute | solution.py:24
  14.2 26.1 %copy-start.4 = (bf16[9,2,96]{2,1,0:T(2,128)(2,1)S(1)}, bf16[9,2,96]{2,1,0:T(2,128)(2,1)}, u32[]{:S(2)}) copy-start(bf16[9,2,96]{2,1,0:T(2,128)(2,1)} %param.23) | copy-start | bytes 10372
  40.4 12.4 %copy-start.1 = (f32[4,2,8,256]{3,2,1,0:T(8,128)S(1)}, f32[4,2,8,256]{3,2,1,0:T(8,128)}, u32[]{:S(2)}) copy-start(f32[4,2,8,256]{3,2,1,0:T(8,128)} %param.19) | copy-start | bytes 196612
  40.4 12.4 %copy-start.6 = (s32[1,1,256]{2,1,0:T(1,128)S(1)}, s32[1,1,256]{2,1,0:T(1,128)}, u32[]{:S(2)}) copy-start(s32[1,1,256]{2,1,0:T(1,128)} %param.28) | copy-start | bytes 3076
  40.4 12.8 %copy-start.5 = (f32[1,1,256]{2,1,0:T(1,128)S(1)}, f32[1,1,256]{2,1,0:T(1,128)}, u32[]{:S(2)}) copy-start(f32[1,1,256]{2,1,0:T(1,128)} %param.29) | copy-start | bytes 3076
  40.4 13.2 %copy-start.2 = (f32[4,2,8,256]{3,2,1,0:T(8,128)S(1)}, f32[4,2,8,256]{3,2,1,0:T(8,128)}, u32[]{:S(2)}) copy-start(f32[4,2,8,256]{3,2,1,0:T(8,128)} %param.20) | copy-start | bytes 196612
  53.6 5.5 %collective-permute-start.4 = (bf16[4,2,8,256]{3,2,1,0:T(8,128)(2,1)S(1)}, bf16[4,2,8,256]{3,2,1,0:T(8,128)(2,1)S(1)}, u32[]{:S(2)}, u32[]{:S(2)}) collective-permute-start(bf16[4,2,8,256]{3,2,1,0:T(8,128)(2,1)S(1)} %get-tuple-element.181), channel_id=1, source_target_pairs={{0,2},{2,4},{4,6},{6,8},{8,10},{10,12},{12,14},{14,16},{16,18},{18... | collective-permute-start | bytes 98312 | tf_op jit(solution)/shard_map/ppermute | solution.py:22
  57.0 6.1 %collective-permute-start.5 = (bf16[4,2,8,256]{3,2,1,0:T(8,128)(2,1)S(1)}, bf16[4,2,8,256]{3,2,1,0:T(8,128)(2,1)S(1)}, u32[]{:S(2)}, u32[]{:S(2)}) collective-permute-start(bf16[4,2,8,256]{3,2,1,0:T(8,128)(2,1)S(1)} %get-tuple-element.181), channel_id=1, source_target_pairs={{2,0},{4,2},{6,4},{8,6},{10,8},{12,10},{14,12},{16,14},{18,16},{20... | collective-permute-start | bytes 98312 | tf_op jit(solution)/shard_map/ppermute | solution.py:24
  63.2 2.7 %collective-permute-start.6 = (bf16[12,2,2,256]{3,2,1,0:T(2,128)(2,1)S(1)}, bf16[12,2,2,256]{3,2,1,0:T(2,128)(2,1)S(1)}, u32[]{:S(2)}, u32[]{:S(2)}) collective-permute-start(bf16[12,2,2,256]{3,2,1,0:T(2,128)(2,1)S(1)} %get-tuple-element.231), channel_id=1, source_target_pairs={{0,1},{1,0},{2,3},{3,2},{4,5},{5,4},{6,7},{7,6},{8,9},{9,8},{10,11... | collective-permute-start | bytes 73736 | tf_op jit(solution)/shard_map/ppermute | solution.py:22
  64.4 2.7 %collective-permute-start.7 = (bf16[12,2,2,256]{3,2,1,0:T(2,128)(2,1)S(1)}, bf16[12,2,2,256]{3,2,1,0:T(2,128)(2,1)S(1)}, u32[]{:S(2)}, u32[]{:S(2)}) collective-permute-start(bf16[12,2,2,256]{3,2,1,0:T(2,128)(2,1)S(1)} %get-tuple-element.232), channel_id=1, source_target_pairs={{1,0},{0,1},{3,2},{2,3},{5,4},{4,5},{7,6},{6,7},{9,8},{8,9},{11,10... | collective-permute-start | bytes 73736 | tf_op jit(solution)/shard_map/ppermute | solution.py:24
  92.0 13.2 %copy-start.3 = (f32[4,2,8,256]{3,2,1,0:T(8,128)S(1)}, f32[4,2,8,256]{3,2,1,0:T(8,128)}, u32[]{:S(2)}) copy-start(f32[4,2,8,256]{3,2,1,0:T(8,128)} %param.21) | copy-start | bytes 196612
where the time goes:
time: 106 us
  matrix products  45.4 us (43%)
  loops' own time  16.3 us (15%)
  local copies, waits for them, and re-layouts  15.7 us (15%)
  starting transfers between devices  14.1 us (13%)
  waiting for transfers between devices  10.7 us (10%)
  other arithmetic  2.59 us (2%)
    dot_general x144, matrix products, conv_three(): jnp.einsum('oc,crw->orw', weights[3 * row_off + col_off], shifted, prefer...  43.8 us
    another operation x2, loops' own time, denoise_net(): hidden = lax.map(hidden_at, jnp.arange(frames_here, dtype=jnp.int32))  15.9 us
    ppermute x4, waiting for transfers between devices, with_halo(): lax.ppermute(head, axis, [((i + 1) % count, i) for i in range(ends)])  9.52 us
    ppermute x4, starting transfers between devices, with_halo(): lax.ppermute(tail, axis, [(i, (i + 1) % count) for i in range(ends)])  8.63 us
    slice x32, local copies, waits for them, and re-layouts, conv_three(): jnp.roll(window[:, row_off:row_off + out_rows, :], 1 - col_off, axis=2)  8.59 us
    ppermute x4, starting transfers between devices, with_halo(): lax.ppermute(head, axis, [((i + 1) % count, i) for i in range(ends)])  5.5 us
    dynamic_slice x8, local copies, waits for them, and re-layouts, denoise_net(): hidden = lax.map(hidden_at, jnp.arange(frames_here, dtype=jnp.int32))  5.02 us
  transfers between devices with their start and end apart: 8, of which 5 were waited for; matrix products, arithmetic and copies ran while one was open for 1% of the time, Pallas kernels for 0%

commit v1 on v0

v1 whole, which is shorter than its diff:
```python
import functools

import jax
import jax.numpy as jnp
from jax import lax
from jax.experimental import pallas as pl
from jax.experimental.pallas import tpu as pltpu
from jax.sharding import PartitionSpec as P

LEVELS = (1.0, 0.5, 0.2)
OBS_NOISE = 0.1
COVARIANCE_GAIN = 0.5

FL = 8
ROWS = 8
COLS = 256
HID = 96
FRAMES = 4
GROUP = 3 * FL
BLOCK = 80
DEPTH = 256
MSG_NOISE = ROWS * FL
MSG_OBS = MSG_NOISE + 4 * FL
MSG_ROWS = MSG_OBS + 16
NO_CELL = 64.0
VMEM = pl.BlockSpec(memory_space=pltpu.VMEM)
SMEM = pl.BlockSpec(memory_space=pltpu.SMEM)
F32 = jnp.float32
BF16 = jnp.bfloat16


def params():
    return pltpu.CompilerParams(vmem_limit_bytes=16 * 1024 * 1024)


def iota(shape, dim):
    return lax.broadcasted_iota(jnp.int32, shape, dim)


def split_halves(ref, halves_ref):
    halves_ref[0 : ROWS * FL, :] = ref[:, 0:128]
    halves_ref[ROWS * FL :, :] = ref[:, 128:256]


def row_of(halves_ref, row):
    left = halves_ref[pl.ds(row, FL, stride=ROWS), :]
    right = halves_ref[pl.ds(ROWS * FL + row, FL, stride=ROWS), :]
    return jnp.concatenate([left, right], axis=1)


def pack_kernel(
    count_ref, x_in, noise_in, step_ref, row_ref, col_ref, val_ref, msg_ref, x_ref, noise_ref
):
    split_halves(x_in, x_ref)
    split_halves(noise_in, noise_ref)
    inv = 1.0 / (1.0 + LEVELS[0] ** 2) ** 0.5
    for row in range(0, ROWS, 2):
        pair = jnp.concatenate([row_of(x_ref, row), row_of(x_ref, row + 1)], axis=0)
        msg_ref[row * FL : (row + 2) * FL, :] = (pair * inv).astype(BF16)
    for at, row in enumerate((0, ROWS - 2)):
        pair = jnp.concatenate([row_of(noise_ref, row), row_of(noise_ref, row + 1)], axis=0)
        msg_ref[MSG_NOISE + 2 * at * FL : MSG_NOISE + 2 * (at + 1) * FL, :] = pair.astype(BF16)
    live = iota((1, COLS), 1) < count_ref[0, 0]
    cell = (row_ref[...] * FL + step_ref[...] * 2).astype(F32)
    cell = jnp.where(live, cell, NO_CELL)
    val = val_ref[...]
    high = val.astype(BF16).astype(F32)
    middle = (val - high).astype(BF16).astype(F32)
    low = val - high - middle
    which = iota((16, COLS), 0)
    table = jnp.zeros((16, COLS), F32)
    for at, line in enumerate((cell, col_ref[...].astype(F32), high, middle, low)):
        table = jnp.where(which == at, line, table)
    msg_ref[MSG_OBS : MSG_OBS + 16, :] = table.astype(BF16)


def weights_kernel(conv_in_ref, conv_out_ref, embed_ref, w1_ref, w2_ref, wide_ref):
    halves = [jnp.zeros((HID, 128), F32), jnp.zeros((HID, 128), F32)]
    wide_ref[...] = jnp.zeros((HID, 128), F32)
    for at in range(9):
        wide_ref[:, 0:18] = conv_in_ref[at].astype(F32)
        start = BLOCK * (at // 3) + GROUP * (at % 3)
        shifted = wide_ref[...]
        if start % 128:
            shifted = pltpu.roll(shifted, start % 128, 1)
        halves[start // 128] = halves[start // 128] + shifted
    square = iota((HID, 128), 0) == iota((HID, 128), 1)
    line = jnp.concatenate([embed_ref[...], jnp.zeros((1, 128 - HID), F32)], axis=1)
    embed = jnp.sum(jnp.where(square, line, 0.0), axis=1, keepdims=True)
    high = embed.astype(BF16).astype(F32)
    middle = (embed - high).astype(BF16).astype(F32)
    low = embed - high - middle
    lane = iota((HID, 128), 1)
    bias = jnp.where(lane == 3 * GROUP, high, 0.0)
    bias = jnp.where(lane == 3 * GROUP + 1, middle, bias)
    bias = jnp.where(lane == 3 * GROUP + 2, low, bias)
    for frame in range(FRAMES):
        left, right = halves
        if frame:
            left = pltpu.roll(left, 2 * frame, 1)
            right = pltpu.roll(right, 2 * frame, 1)
        rows = slice(frame * HID, (frame + 1) * HID)
        w1_ref[rows, 0:128] = (0.5 * (left + bias)).astype(BF16)
        w1_ref[rows, 128:256] = (0.5 * right).astype(BF16)
    odd = iota((FL, HID), 0) % 2 == 1
    parts = []
    for at in range(9):
        upper = conv_out_ref[at, 0:1, :].astype(F32)
        lower = conv_out_ref[at, 1:2, :].astype(F32)
        parts.append(jnp.where(odd, lower, upper))
    stacked = jnp.concatenate(parts, axis=0).astype(BF16)
    shape = (HID, FRAMES * HID)
    spread = jnp.where(iota(shape, 1) % HID == iota(shape, 0), 1.0, 0.0).astype(BF16)
    tiled = jnp.dot(stacked, spread, preferred_element_type=F32)
    mine = (iota(tiled.shape, 0) % FL) // 2 == iota(tiled.shape, 1) // HID
    w2_ref[...] = jnp.where(mine, tiled, 0.0).astype(BF16)


def one_hot_maps(table, first_cell, cells):
    shape = (cells, COLS)
    hit = (iota(shape, 0) + first_cell).astype(F32) == table[0:1, :]
    lines = [jnp.where(hit, 1.0, 0.0)]
    for at in (2, 3, 4):
        lines.append(jnp.where(hit, table[at : at + 1, :], 0.0))
    lhs = jnp.concatenate(lines, axis=0).astype(BF16)
    cols_hot = jnp.where(iota((COLS, COLS), 0).astype(F32) == table[1:2, :], 1.0, 0.0)
    out = lax.dot_general(
        lhs, cols_hot.astype(BF16), (((1,), (1,)), ((), ())), preferred_element_type=F32
    )
    count = out[0:cells]
    total = out[cells : 2 * cells] + out[2 * cells : 3 * cells] + out[3 * cells : 4 * cells]
    return count, total


def maps_kernel(msg_ref, up_ref, down_ref, count_ref, total_ref):
    obs = slice(MSG_OBS, MSG_OBS + 16)
    pieces = (
        (up_ref, (ROWS - 2) * FL, 2 * FL, 0),
        (msg_ref, 0, ROWS * FL, 2 * FL),
        (down_ref, 0, 2 * FL, (ROWS + 2) * FL),
    )
    for ref, first_cell, cells, at in pieces:
        count, total = one_hot_maps(ref[obs, :].astype(F32), first_cell, cells)
        count_ref[at : at + cells, :] = count
        total_ref[at : at + cells, :] = total


def fill_windows(flags_ref, core_ref, own_ref, far_ref, win_ref, rows, level):
    even = flags_ref[0] == 1
    has_prev = flags_ref[1] == 1
    has_next = flags_ref[2] == 1
    const = jnp.full((FL, COLS), level, F32)
    for row in range(0, rows, 2):
        at = slice(row * FL, (row + 2) * FL)
        core = core_ref[at, :].astype(F32)
        own = own_ref[at, :].astype(F32)
        far = far_ref[at, :].astype(F32)
        prev = jnp.where(has_prev, jnp.where(even, far, core), 0.0)
        nxt = jnp.where(has_next, jnp.where(even, core, far), 0.0)
        for sub in range(2):
            part = slice(sub * FL, (sub + 1) * FL)
            here = jnp.concatenate([prev[part], own[part], nxt[part]], axis=0)
            block = jnp.concatenate(
                [pltpu.roll(here, 1, 1), here, pltpu.roll(here, COLS - 1, 1), const], axis=0
            )
            win_ref[(row + sub) * BLOCK : (row + sub + 1) * BLOCK, :] = block.astype(BF16)
    win_ref[rows * BLOCK : rows * BLOCK + 16, :] = jnp.zeros((16, COLS), BF16)


def hidden_products(w1_ref, w2_ref, win_ref, prod_ref, hidden_rows):
    def one_row(row, carry):
        start = pl.multiple_of(row * BLOCK, 16)
        half = jnp.dot(w1_ref[...], win_ref[pl.ds(start, DEPTH), :], preferred_element_type=F32)
        hidden = (half + half * jnp.tanh(half)).astype(BF16)
        out = jnp.dot(w2_ref[...], hidden, preferred_element_type=F32)
        prod_ref[pl.ds(pl.multiple_of(row * 72, 8), 72), :] = out
        return carry

    lax.fori_loop(0, hidden_rows, one_row, 0, unroll=2)


def net_row(prod_ref, row):
    sums = []
    for col_off in range(3):
        acc = None
        for row_off in range(3):
            at = (row + row_off) * 72 + (3 * row_off + col_off) * FL
            term = prod_ref[at : at + FL, :]
            acc = term if acc is None else acc + term
        sums.append(acc)
    return pltpu.roll(sums[0], 1, 1) + sums[1] + pltpu.roll(sums[2], COLS - 1, 1)


def advance(x, noise, net, count, total, index):
    level, after = LEVELS[index], LEVELS[index + 1]
    spread = level**2 - after**2
    denoised = x * (1.0 / (1.0 + level**2)) + (level / (1.0 + level**2) ** 0.5) * net
    guide = (total - count * denoised) * (1.0 / (OBS_NOISE + COVARIANCE_GAIN * level**2))
    score = (denoised - x) * (1.0 / level**2) + guide
    return x + spread * score + spread**0.5 * noise


def first_kernel(
    flags_ref, x_in, noise_in, up_ref, down_ref, core_ref, own_ref, far_ref, w1_ref, w2_ref,
    count_ref, total_ref, next_ref, send_ref, win_ref, prod_ref, x_ref, noise_ref,
):
    rows = 2 * ROWS
    split_halves(x_in, x_ref)
    split_halves(noise_in, noise_ref)
    fill_windows(flags_ref, core_ref, own_ref, far_ref, win_ref, rows, LEVELS[0])
    hidden_products(w1_ref, w2_ref, win_ref, prod_ref, rows - 2)
    grow = (1.0 + LEVELS[0] ** 2) ** 0.5
    shrink = 1.0 / (1.0 + LEVELS[1] ** 2) ** 0.5
    for row in range(0, ROWS + 4, 2):
        both = []
        if row == 0:
            x_pair = up_ref[(ROWS - 2) * FL : ROWS * FL, :].astype(F32) * grow
            noise_pair = up_ref[MSG_NOISE + 2 * FL : MSG_NOISE + 4 * FL, :].astype(F32)
        elif row == ROWS + 2:
            x_pair = down_ref[0 : 2 * FL, :].astype(F32) * grow
            noise_pair = down_ref[MSG_NOISE : MSG_NOISE + 2 * FL, :].astype(F32)
        for sub in range(2):
            part = slice(sub * FL, (sub + 1) * FL)
            here = row + sub
            inside = 2 <= here < ROWS + 2
            x = row_of(x_ref, here - 2) if inside else x_pair[part]
            noise = row_of(noise_ref, here - 2) if inside else noise_pair[part]
            at = slice(here * FL, (here + 1) * FL)
            new = advance(
                x, noise, net_row(prod_ref, here), count_ref[at, :], total_ref[at, :], 0
            )
            if inside:
                next_ref[(here - 2) * FL : (here - 1) * FL, :] = new
            both.append(new)
        pair = jnp.concatenate(both, axis=0) * shrink
        send_ref[row * FL : (row + 2) * FL, :] = pair.astype(BF16)


def second_kernel(
    flags_ref, x_ref, noise_in, core_ref, own_ref, far_ref, w1_ref, w2_ref,
    count_ref, total_ref, out_ref, win_ref, prod_ref, noise_ref, half_ref,
):
    rows = ROWS + 4
    split_halves(noise_in, noise_ref)
    fill_windows(flags_ref, core_ref, own_ref, far_ref, win_ref, rows, LEVELS[1])
    hidden_products(w1_ref, w2_ref, win_ref, prod_ref, rows - 2)
    for row in range(ROWS):
        at = slice((row + 2) * FL, (row + 3) * FL)
        new = advance(
            x_ref[row * FL : (row + 1) * FL, :], row_of(noise_ref, row), net_row(prod_ref, row),
            count_ref[at, :], total_ref[at, :], 1,
        )
        half_ref[pl.ds(row, FL, stride=ROWS), :] = new[:, 0:128]
        half_ref[pl.ds(ROWS * FL + row, FL, stride=ROWS), :] = new[:, 128:256]
    out_ref[:, 0:128] = half_ref[0 : ROWS * FL, :]
    out_ref[:, 128:256] = half_ref[ROWS * FL :, :]


def call(kernel, args, specs, outs, scratch=(), name=None, flops=0):
    moved = sum(a.size * a.dtype.itemsize for a in args)
    moved += sum(o.size * o.dtype.itemsize for o in outs)
    return pl.pallas_call(
        kernel,
        out_shape=tuple(outs),
        in_specs=specs,
        out_specs=tuple([VMEM] * len(outs)),
        scratch_shapes=list(scratch),
        compiler_params=params(),
        cost_estimate=pl.CostEstimate(flops=flops, bytes_accessed=moved, transcendentals=0),
        name=name,
    )(*args)


def time_pairs(n_tm, n_rows):
    core, far = [], []
    at = lambda i, r: i * n_rows + r
    for r in range(n_rows):
        for i in range(0, n_tm, 2):
            core += [(at(i, r), at(i + 1, r)), (at(i + 1, r), at(i, r))]
        for i in range(1, n_tm - 1, 2):
            far += [(at(i, r), at(i + 1, r)), (at(i + 1, r), at(i, r))]
        for i in (0, n_tm - 1):
            far.append((at(i, r), at(i, r ^ 1)))
    return core, far


def exchange_time(block, n_tm, n_rows):
    core, far = time_pairs(n_tm, n_rows)
    return (
        lax.ppermute(block, ("tm", "rows"), core),
        lax.ppermute(block, ("tm", "rows"), far),
    )


def per_device(
    noisy_states, noise_first, noise_second, conv_in, conv_out, level_embed,
    obs_count, obs_step, obs_row, obs_col, obs_value,
):
    n_tm, n_rows = lax.axis_size("tm"), lax.axis_size("rows")
    frames, layers, rows, cols = noisy_states.shape
    assert frames == FRAMES and frames * layers == FL and rows == ROWS and cols == COLS
    assert n_tm % 2 == 0 and n_rows % 2 == 0 and obs_step.shape[-1] == COLS
    flat = lambda a: a.reshape(FL * ROWS, COLS)
    line = lambda a: a.reshape(1, -1)
    x, noise_a, noise_b = flat(noisy_states), flat(noise_first), flat(noise_second)
    shape = jax.ShapeDtypeStruct
    here = lax.axis_index("tm")
    flags = jnp.stack(
        [
            (here % 2 == 0).astype(jnp.int32),
            (here > 0).astype(jnp.int32),
            (here < n_tm - 1).astype(jnp.int32),
        ]
    )

    halves = pltpu.VMEM((2 * ROWS * FL, 128), F32)
    (msg,) = call(
        pack_kernel,
        (obs_count, x, noise_a, line(obs_step), line(obs_row), line(obs_col), line(obs_value)),
        [SMEM] + [VMEM] * 6,
        [shape((MSG_ROWS, COLS), BF16)],
        [halves, halves],
        name="pack",
    )
    up = lax.ppermute(msg, "rows", [(i, (i + 1) % n_rows) for i in range(n_rows)])
    if n_rows == 2:
        down = up
    else:
        down = lax.ppermute(msg, "rows", [((i + 1) % n_rows, i) for i in range(n_rows)])
    w1, w2 = call(
        weights_kernel,
        (conv_in, conv_out, line(level_embed)),
        [VMEM] * 3,
        [shape((FRAMES * HID, DEPTH), BF16), shape((72, FRAMES * HID), BF16)],
        [pltpu.VMEM((HID, 128), F32)],
        name="weights",
    )
    half = ROWS * FL // 2
    own = jnp.concatenate([up[half : 2 * half], msg[: 2 * half], down[:half]], axis=0)
    core, far = exchange_time(own, n_tm, n_rows)
    maps = shape(((ROWS + 4) * FL, COLS), F32)
    count, total = call(maps_kernel, (msg, up, down), [VMEM] * 3, [maps, maps], name="maps")
    scratch = lambda n: [
        pltpu.VMEM((n * BLOCK + 16, COLS), BF16),
        pltpu.VMEM(((n - 2) * 72, COLS), F32),
        halves,
        halves,
    ]
    current, send = call(
        first_kernel,
        (flags, x, noise_a, up, down, core, own, far, w1, w2, count, total),
        [SMEM] + [VMEM] * 11,
        [shape((ROWS * FL, COLS), F32), shape(((ROWS + 4) * FL, COLS), BF16)],
        scratch(2 * ROWS),
        name="first",
        flops=14 * 2 * 256 * 384 * (256 + 72),
    )
    core, far = exchange_time(send, n_tm, n_rows)
    (out,) = call(
        second_kernel,
        (flags, current, noise_b, core, send, far, w1, w2, count, total),
        [SMEM] + [VMEM] * 9,
        [shape((FL * ROWS, COLS), F32)],
        scratch(ROWS + 4),
        name="second",
        flops=10 * 2 * 256 * 384 * (256 + 72),
    )
    return out.reshape(noisy_states.shape)


def solution(mesh):
    states = P("tm", None, "rows", None)
    slots = P("tm", "rows", None)
    in_specs = (states, states, states, P(), P(), P(), P("tm", "rows"), slots, slots, slots, slots)
    return jax.shard_map(
        per_device, mesh=mesh, in_specs=in_specs, out_specs=states, check_vma=False
    )
```

time: 106 us -> 27.9 us (0.26)
  matrix products: 45.4 us -> 0 us
  loops' own time: 16.3 us -> 0 us
  local copies, waits for them, and re-layouts: 15.7 us -> 3.72 us
  Pallas kernels: 0 us -> 11 us
  starting transfers between devices: 14.1 us -> 4.91 us
  waiting for transfers between devices: 10.7 us -> 7.18 us
  other arithmetic: 2.59 us -> 0.08 us
    dot_general x148 -> x0, matrix products: 45.4 us -> none  [the longest x144 43.8 us: conv_three(): jnp.einsum('oc,crw->orw', weights[3 * row_off + col_off], shifted, prefer...]
    another operation x4 -> x0, loops' own time: 16.3 us -> none  [the longest x2 15.9 us: denoise_net(): hidden = lax.map(hidden_at, jnp.arange(frames_here, dtype=jnp.int32))]
    pallas_call x0 -> x5, Pallas kernels: none -> 11 us  [call(): pl.pallas_call(kernel, out_shape=tuple(outs), in_specs=specs, out_specs=t...]
    ppermute x8 -> x5, starting transfers between devices: 14.1 us -> 4.91 us  [the longest x2 2.62 us: exchange_time(): lax.ppermute(block, ('tm', 'rows'), far)]
    slice x32 -> x2, local copies, waits for them, and re-layouts: 8.59 us -> 0.01 us  [the longest x1 0.01 us: per_device(): msg[:2 * half]]
    dynamic_slice x16 -> x0, local copies, waits for them, and re-layouts: 5.69 us -> none  [the longest x8 5.02 us: denoise_net(): hidden = lax.map(hidden_at, jnp.arange(frames_here, dtype=jnp.int32))]
    unnamed x16 -> x25, local copies, waits for them, and re-layouts: 0.05 us -> 3.72 us
    ppermute x8 -> x5, waiting for transfers between devices: 10.7 us -> 7.18 us  [the longest x2 6.07 us: exchange_time(): lax.ppermute(block, ('tm', 'rows'), far)]
  transfers between devices with their start and end apart: 8 -> 5, of which waited for: 5 -> 3; matrix products, arithmetic and copies ran while one was open for 1% -> 1% of each run, Pallas kernels for 0% -> 2%
where the time goes in v1:
time: 27.9 us; the launch traced here: 27.7 us
  Pallas kernels  11 us (39%)
  waiting for transfers between devices  7.18 us (26%)
  starting transfers between devices  4.91 us (18%)
  local copies, waits for them, and re-layouts  3.72 us (13%)
  between operations  0.75 us (3%)
    pallas_call x5, Pallas kernels, call(): pl.pallas_call(kernel, out_shape=tuple(outs), in_specs=specs, out_specs=t...  11 us
    ppermute x2, waiting for transfers between devices, exchange_time(): lax.ppermute(block, ('tm', 'rows'), far)  6.07 us
    unnamed x25, local copies, waits for them, and re-layouts  3.72 us
    ppermute x2, starting transfers between devices, exchange_time(): lax.ppermute(block, ('tm', 'rows'), far)  2.62 us
    ppermute x2, starting transfers between devices, exchange_time(): lax.ppermute(block, ('tm', 'rows'), core)  1.96 us
    ppermute x1, waiting for transfers between devices, per_device(): lax.ppermute(msg, 'rows', [(i, (i + 1) % n_rows) for i in range(n_rows)])  1.1 us
  transfers between devices with their start and end apart: 5, of which 3 were waited for; matrix products, arithmetic and copies ran while one was open for 1% of the time, Pallas kernels for 2%

profile of v1, /device:TPU:15, one launch (start us, length us, event | category | flops | bytes accessed | tf_op | source)
XLA Modules:
  0.0 27.7 jit_solution(10590707099871275092)
XLA Ops:
  0.7 0.0 copy-start.8
  0.7 0.0 copy-start.6
  0.7 0.0 copy-start.7
  0.7 0.0 copy-start.5
  0.7 0.6 %copy-done.8 = f32[1,1,256]{2,1,0:T(1,128)S(1)} copy-done((f32[1,1,256]{2,1,0:T(1,128)S(1)}, f32[1,1,256]{2,1,0:T(1,128)}, u32[]{:S(2)}) %copy-start.8) | copy-done | bytes 1048
  1.3 0.0 copy-done.6
  1.3 0.0 copy-done.7
  1.4 0.0 copy-done.5
  1.4 0.0 copy-start
  1.4 0.8 %copy-done = f32[4,2,8,256]{3,2,1,0:T(8,128)S(1)} copy-done((f32[4,2,8,256]{3,2,1,0:T(8,128)S(1)}, f32[4,2,8,256]{3,2,1,0:T(8,128)}, u32[]{:S(2)}) %copy-start) | copy-done | bytes 65560
  2.2 0.0 copy-start.2
  2.2 0.8 %copy-done.2 = f32[4,2,8,256]{3,2,1,0:T(8,128)S(1)} copy-done((f32[4,2,8,256]{3,2,1,0:T(8,128)S(1)}, f32[4,2,8,256]{3,2,1,0:T(8,128)}, u32[]{:S(2)}) %copy-start.2) | copy-done | bytes 65560
  3.1 0.0 copy-start.11
  3.1 0.3 %collective-permute-start = (bf16[112,256]{1,0:T(8,128)(2,1)S(1)}, bf16[112,256]{1,0:T(8,128)(2,1)S(1)}, u32[]{:S(2)}, u32[]{:S(2)}) collective-permute-start(bf16[112,256]{1,0:T(8,128)(2,1)S(1)} %pack.1.msg_ref), channel_id=1, source_target_pairs={{0,1},{1,0},{2,3},{3,2},{4,5},{5,4},{6,7},{7,6},{8,9},{9,8},{10,11... | collective-permute-start | bytes 172040 | tf_op jit(solution)/shard_map/ppermute | solution.py:325
  3.4 0.5 %copy-done.11 = bf16[9,96,18]{1,2,0:T(8,128)(2,1)S(1)} copy-done((bf16[9,96,18]{1,2,0:T(8,128)(2,1)S(1)}, bf16[9,96,18]{1,2,0:T(8,128)(2,1)}, u32[]{:S(2)}) %copy-start.11) | copy-done | bytes 31128
  3.9 0.0 copy-start.4
  3.9 0.2 copy.12.conv_in_ref
  4.1 0.0 copy-start.9
  4.1 0.5 %copy-done.4 = bf16[9,2,96]{2,1,0:T(2,128)(2,1)S(1)} copy-done((bf16[9,2,96]{2,1,0:T(2,128)(2,1)S(1)}, bf16[9,2,96]{2,1,0:T(2,128)(2,1)}, u32[]{:S(2)}) %copy-start.4) | copy-done | bytes 3480
  4.6 0.2 copy-done.9
  4.8 0.3 %weights.1 = (bf16[384,256]{1,0:T(8,128)(2,1)S(1)}, bf16[72,384]{1,0:T(8,128)(2,1)S(1)}) custom-call(bf16[9,96,18]{2,1,0:T(8,128)(2,1)S(1)} %copy.12.conv_in_ref, bf16[9,2,96]{2,1,0:T(2,128)(2,1)S(1)} %copy-done.4, f32[1,96]{1,0:T(1,128)S(1)} %bitcast.20), custom_call_target="tpu_custom_call" | custom-call | bytes 286848 | tf_op jit(solution)/shard_map/weights/pallas_call | solution.py:262
  5.1 1.1 %collective-permute-done.up_ref.down_ref = bf16[112,256]{1,0:T(8,128)(2,1)S(1)} collective-permute-done((bf16[112,256]{1,0:T(8,128)(2,1)S(1)}, bf16[112,256]{1,0:T(8,128)(2,1)S(1)}, u32[]{:S(2)}, u32[]{:S(2)}) %collective-permute-start) | collective-permute-done | bytes 57376 | tf_op jit(solution)/shard_map/ppermute | solution.py:325
  6.2 1.9 %collective-permute-start.1 = (bf16[128,256]{1,0:T(8,128)(2,1)S(1)}, bf16[128,256]{1,0:T(8,128)(2,1)S(1)}, u32[]{:S(2)}, u32[]{:S(2)}) collective-permute-start(bf16[128,256]{1,0:T(8,128)(2,1)S(1)} %pad_maximum_fusion.own_ref), channel_id=1, source_target_pairs={{0,2},{2,0},{4,6},{6,4},{8,10},{10,8},{12,14},{14,12},{16,18},{18,... | collective-permute-start | bytes 196616 | tf_op jit(solution)/shard_map/ppermute | solution.py:290
  8.1 1.2 %collective-permute-start.2 = (bf16[128,256]{1,0:T(8,128)(2,1)S(1)}, bf16[128,256]{1,0:T(8,128)(2,1)S(1)}, u32[]{:S(2)}, u32[]{:S(2)}) collective-permute-start(bf16[128,256]{1,0:T(8,128)(2,1)S(1)} %pad_maximum_fusion.own_ref), channel_id=1, source_target_pairs={{2,4},{4,2},{6,8},{8,6},{10,12},{12,10},{14,16},{16,14},{18,20},{2... | collective-permute-start | bytes 196616 | tf_op jit(solution)/shard_map/ppermute | solution.py:291
  9.3 0.1 add_convert_fusion.flags_ref
  9.4 0.0 copy-start.1
  9.4 0.0 copy-start.3
  9.4 0.3 maps.1
  9.7 0.0 collective-permute-done.1.core_ref
  9.7 3.0 %collective-permute-done.2.far_ref = bf16[128,256]{1,0:T(8,128)(2,1)S(1)} collective-permute-done((bf16[128,256]{1,0:T(8,128)(2,1)S(1)}, bf16[128,256]{1,0:T(8,128)(2,1)S(1)}, u32[]{:S(2)}, u32[]{:S(2)}) %collective-permute-start.2) | collective-permute-done | bytes 65568 | tf_op jit(solution)/shard_map/ppermute | solution.py:291
  12.7 0.0 copy-done.1
  12.7 0.0 copy-done.3
  12.7 0.0 copy-start.10
  12.7 5.6 %first.1 = (f32[64,256]{1,0:T(8,128)S(1)}, bf16[96,256]{1,0:T(8,128)(2,1)S(1)}) custom-call(s32[3]{0:T(128)S(1)} %add_convert_fusion.flags_ref, f32[64,256]{1,0:T(8,128)S(1)} %bitcast.13, f32[64,256]{1,0:T(8,128)S(1)} %bitcast.15, bf16[112,256]{1,0:T(8,128)(2,1)S(1)} %collective-permute-done.up_ref.down_ref, ...), custom_call_target="tpu_custom_call" | custom-call | flops 902823936 | bytes 1005580 | tf_op jit(solution)/shard_map/first/pallas_call | solution.py:262
  18.3 0.1 collective-permute-start.3
  18.4 1.4 %collective-permute-start.4 = (bf16[96,256]{1,0:T(8,128)(2,1)S(1)}, bf16[96,256]{1,0:T(8,128)(2,1)S(1)}, u32[]{:S(2)}, u32[]{:S(2)}) collective-permute-start(bf16[96,256]{1,0:T(8,128)(2,1)S(1)} %get-tuple-element.16.own_ref), channel_id=1, source_target_pairs={{2,4},{4,2},{6,8},{8,6},{10,12},{12,10},{14,16},{16,14},{18,20},{2... | collective-permute-start | bytes 147464 | tf_op jit(solution)/shard_map/ppermute | solution.py:291
  19.8 0.0 collective-permute-done.3.core_ref
  19.8 3.1 %collective-permute-done.4.far_ref = bf16[96,256]{1,0:T(8,128)(2,1)S(1)} collective-permute-done((bf16[96,256]{1,0:T(8,128)(2,1)S(1)}, bf16[96,256]{1,0:T(8,128)(2,1)S(1)}, u32[]{:S(2)}, u32[]{:S(2)}) %collective-permute-start.4) | collective-permute-done | bytes 49184 | tf_op jit(solution)/shard_map/ppermute | solution.py:291
  22.8 0.0 copy-done.10
  22.8 4.8 %second.1 = f32[64,256]{1,0:T(8,128)} custom-call(s32[3]{0:T(128)S(1)} %add_convert_fusion.flags_ref, f32[64,256]{1,0:T(8,128)S(1)} %get-tuple-element.15.x_ref, f32[64,256]{1,0:T(8,128)S(1)} %bitcast.21, bf16[96,256]{1,0:T(8,128)(2,1)S(1)} %collective-permute-done.3.core_ref, bf16[96,256]{1,0:T(8,128)(2,1)S(1)} %get-tuple-element.16.own_ref, ...), custom_call_target="tpu_custom_call" | custom-call | flops 644874240 | bytes 792588 | tf_op jit(solution)/shard_map/second/pallas_call | solution.py:262
  (4 shorter events, 0.1 us)
Async XLA Ops:
  0.7 0.7 %copy-start.8 = (f32[1,1,256]{2,1,0:T(1,128)S(1)}, f32[1,1,256]{2,1,0:T(1,128)}, u32[]{:S(2)}) copy-start(f32[1,1,256]{2,1,0:T(1,128)} %param.21) | copy-start | bytes 3076
  0.7 0.7 %copy-start.6 = (s32[1,1,256]{2,1,0:T(1,128)S(1)}, s32[1,1,256]{2,1,0:T(1,128)}, u32[]{:S(2)}) copy-start(s32[1,1,256]{2,1,0:T(1,128)} %param.19) | copy-start | bytes 3076
  0.7 0.7 %copy-start.7 = (s32[1,1,256]{2,1,0:T(1,128)S(1)}, s32[1,1,256]{2,1,0:T(1,128)}, u32[]{:S(2)}) copy-start(s32[1,1,256]{2,1,0:T(1,128)} %param.20) | copy-start | bytes 3076
  0.7 0.7 %copy-start.5 = (s32[1,1,256]{2,1,0:T(1,128)S(1)}, s32[1,1,256]{2,1,0:T(1,128)}, u32[]{:S(2)}) copy-start(s32[1,1,256]{2,1,0:T(1,128)} %param.18) | copy-start | bytes 3076
  1.4 0.8 %copy-start = (f32[4,2,8,256]{3,2,1,0:T(8,128)S(1)}, f32[4,2,8,256]{3,2,1,0:T(8,128)}, u32[]{:S(2)}) copy-start(f32[4,2,8,256]{3,2,1,0:T(8,128)} %param.11) | copy-start | bytes 196612
  2.2 0.8 %copy-start.2 = (f32[4,2,8,256]{3,2,1,0:T(8,128)S(1)}, f32[4,2,8,256]{3,2,1,0:T(8,128)}, u32[]{:S(2)}) copy-start(f32[4,2,8,256]{3,2,1,0:T(8,128)} %param.12) | copy-start | bytes 196612
  3.1 0.8 %copy-start.11 = (bf16[9,96,18]{1,2,0:T(8,128)(2,1)S(1)}, bf16[9,96,18]{1,2,0:T(8,128)(2,1)}, u32[]{:S(2)}) copy-start(bf16[9,96,18]{1,2,0:T(8,128)(2,1)} %param.14) | copy-start | bytes 93316
  3.1 3.1 %collective-permute-start = (bf16[112,256]{1,0:T(8,128)(2,1)S(1)}, bf16[112,256]{1,0:T(8,128)(2,1)S(1)}, u32[]{:S(2)}, u32[]{:S(2)}) collective-permute-start(bf16[112,256]{1,0:T(8,128)(2,1)S(1)} %pack.1.msg_ref), channel_id=1, source_target_pairs={{0,1},{1,0},{2,3},{3,2},{4,5},{5,4},{6,7},{7,6},{8,9},{9,8},{10,11... | collective-permute-start | bytes 172040 | tf_op jit(solution)/shard_map/ppermute | solution.py:325
  3.9 0.7 %copy-start.4 = (bf16[9,2,96]{2,1,0:T(2,128)(2,1)S(1)}, bf16[9,2,96]{2,1,0:T(2,128)(2,1)}, u32[]{:S(2)}) copy-start(bf16[9,2,96]{2,1,0:T(2,128)(2,1)} %conv_out_ref.1) | copy-start | bytes 10372
  4.1 0.7 %copy-start.9 = (f32[96]{0:T(128)S(1)}, f32[96]{0:T(128)}, u32[]{:S(2)}) copy-start(f32[96]{0:T(128)} %param.16) | copy-start | bytes 1156
  6.2 3.5 %collective-permute-start.1 = (bf16[128,256]{1,0:T(8,128)(2,1)S(1)}, bf16[128,256]{1,0:T(8,128)(2,1)S(1)}, u32[]{:S(2)}, u32[]{:S(2)}) collective-permute-start(bf16[128,256]{1,0:T(8,128)(2,1)S(1)} %pad_maximum_fusion.own_ref), channel_id=1, source_target_pairs={{0,2},{2,0},{4,6},{6,4},{8,10},{10,8},{12,14},{14,12},{16,18},{18,... | collective-permute-start | bytes 196616 | tf_op jit(solution)/shard_map/ppermute | solution.py:290
  8.1 4.6 %collective-permute-start.2 = (bf16[128,256]{1,0:T(8,128)(2,1)S(1)}, bf16[128,256]{1,0:T(8,128)(2,1)S(1)}, u32[]{:S(2)}, u32[]{:S(2)}) collective-permute-start(bf16[128,256]{1,0:T(8,128)(2,1)S(1)} %pad_maximum_fusion.own_ref), channel_id=1, source_target_pairs={{2,4},{4,2},{6,8},{8,6},{10,12},{12,10},{14,16},{16,14},{18,20},{2... | collective-permute-start | bytes 196616 | tf_op jit(solution)/shard_map/ppermute | solution.py:291
  9.4 3.3 %copy-start.1 = (f32[4,2,8,256]{3,2,1,0:T(8,128)S(1)}, f32[4,2,8,256]{3,2,1,0:T(8,128)}, u32[]{:S(2)}) copy-start(f32[4,2,8,256]{3,2,1,0:T(8,128)} %param.11) | copy-start | bytes 196612
  9.4 3.3 %copy-start.3 = (f32[4,2,8,256]{3,2,1,0:T(8,128)S(1)}, f32[4,2,8,256]{3,2,1,0:T(8,128)}, u32[]{:S(2)}) copy-start(f32[4,2,8,256]{3,2,1,0:T(8,128)} %param.12) | copy-start | bytes 196612
  12.7 10.1 %copy-start.10 = (f32[4,2,8,256]{3,2,1,0:T(8,128)S(1)}, f32[4,2,8,256]{3,2,1,0:T(8,128)}, u32[]{:S(2)}) copy-start(f32[4,2,8,256]{3,2,1,0:T(8,128)} %param.13) | copy-start | bytes 196612
  18.3 1.5 %collective-permute-start.3 = (bf16[96,256]{1,0:T(8,128)(2,1)S(1)}, bf16[96,256]{1,0:T(8,128)(2,1)S(1)}, u32[]{:S(2)}, u32[]{:S(2)}) collective-permute-start(bf16[96,256]{1,0:T(8,128)(2,1)S(1)} %get-tuple-element.16.own_ref), channel_id=1, source_target_pairs={{0,2},{2,0},{4,6},{6,4},{8,10},{10,8},{12,14},{14,12},{16,18},{18,... | collective-permute-start | bytes 147464 | tf_op jit(solution)/shard_map/ppermute | solution.py:290
  18.4 4.5 %collective-permute-start.4 = (bf16[96,256]{1,0:T(8,128)(2,1)S(1)}, bf16[96,256]{1,0:T(8,128)(2,1)S(1)}, u32[]{:S(2)}, u32[]{:S(2)}) collective-permute-start(bf16[96,256]{1,0:T(8,128)(2,1)S(1)} %get-tuple-element.16.own_ref), channel_id=1, source_target_pairs={{2,4},{4,2},{6,8},{8,6},{10,12},{12,10},{14,16},{16,14},{18,20},{2... | collective-permute-start | bytes 147464 | tf_op jit(solution)/shard_map/ppermute | solution.py:291

commit v2 on v1

--- a/solution.py
+++ b/solution.py
@@ -23,6 +23,7 @@
 MSG_OBS = MSG_NOISE + 4 * FL
 MSG_ROWS = MSG_OBS + 16
 NO_CELL = 64.0
+AHEAD, LAG2, LAG3 = 4, 3, 3
 VMEM = pl.BlockSpec(memory_space=pltpu.VMEM)
 SMEM = pl.BlockSpec(memory_space=pltpu.SMEM)
 F32 = jnp.float32
@@ -38,8 +39,8 @@
 
 
 def split_halves(ref, halves_ref):
-    halves_ref[0 : ROWS * FL, :] = ref[:, 0:128]
-    halves_ref[ROWS * FL :, :] = ref[:, 128:256]
+    halves_ref[0 : ROWS * FL, :] = ref[:, 0:128].astype(F32)
+    halves_ref[ROWS * FL :, :] = ref[:, 128:256].astype(F32)
 
 
 def row_of(halves_ref, row):
@@ -49,14 +50,13 @@
 
 
 def pack_kernel(
-    count_ref, x_in, noise_in, step_ref, row_ref, col_ref, val_ref, msg_ref, x_ref, noise_ref
+    count_ref, scaled_in, noise_in, step_ref, row_ref, col_ref, val_ref, msg_ref, scaled_ref, noise_ref
 ):
-    split_halves(x_in, x_ref)
+    split_halves(scaled_in, scaled_ref)
     split_halves(noise_in, noise_ref)
-    inv = 1.0 / (1.0 + LEVELS[0] ** 2) ** 0.5
     for row in range(0, ROWS, 2):
-        pair = jnp.concatenate([row_of(x_ref, row), row_of(x_ref, row + 1)], axis=0)
-        msg_ref[row * FL : (row + 2) * FL, :] = (pair * inv).astype(BF16)
+        pair = jnp.concatenate([row_of(scaled_ref, row), row_of(scaled_ref, row + 1)], axis=0)
+        msg_ref[row * FL : (row + 2) * FL, :] = pair.astype(BF16)
     for at, row in enumerate((0, ROWS - 2)):
         pair = jnp.concatenate([row_of(noise_ref, row), row_of(noise_ref, row + 1)], axis=0)
         msg_ref[MSG_NOISE + 2 * at * FL : MSG_NOISE + 2 * (at + 1) * FL, :] = pair.astype(BF16)
@@ -145,38 +145,46 @@
         total_ref[at : at + cells, :] = total
 
 
-def fill_windows(flags_ref, core_ref, own_ref, far_ref, win_ref, rows, level):
-    even = flags_ref[0] == 1
-    has_prev = flags_ref[1] == 1
-    has_next = flags_ref[2] == 1
+def fill_pair(flags, refs, win_ref, pair, level):
+    even, has_prev, has_next = flags
+    at = slice(2 * pair * FL, 2 * (pair + 1) * FL)
+    core, own, far = (ref[at, :].astype(F32) for ref in refs)
+    prev = jnp.where(has_prev, jnp.where(even, far, core), 0.0)
+    nxt = jnp.where(has_next, jnp.where(even, core, far), 0.0)
     const = jnp.full((FL, COLS), level, F32)
-    for row in range(0, rows, 2):
-        at = slice(row * FL, (row + 2) * FL)
-        core = core_ref[at, :].astype(F32)
-        own = own_ref[at, :].astype(F32)
-        far = far_ref[at, :].astype(F32)
-        prev = jnp.where(has_prev, jnp.where(even, far, core), 0.0)
-        nxt = jnp.where(has_next, jnp.where(even, core, far), 0.0)
-        for sub in range(2):
-            part = slice(sub * FL, (sub + 1) * FL)
-            here = jnp.concatenate([prev[part], own[part], nxt[part]], axis=0)
-            block = jnp.concatenate(
-                [pltpu.roll(here, 1, 1), here, pltpu.roll(here, COLS - 1, 1), const], axis=0
+    for sub in range(2):
+        part = slice(sub * FL, (sub + 1) * FL)
+        here = jnp.concatenate([prev[part], own[part], nxt[part]], axis=0)
+        block = jnp.concatenate(
+            [pltpu.roll(here, 1, 1), here, pltpu.roll(here, COLS - 1, 1), const], axis=0
+        )
+        start = (2 * pair + sub) * BLOCK
+        win_ref[start : start + BLOCK, :] = block.astype(BF16)
+
+
+def run_rows(flags_ref, refs, w1_ref, w2_ref, win_ref, hid_ref, prod_ref, rows, level, emit):
+    flags = [flags_ref[at] == 1 for at in range(3)]
+    hidden_rows = rows - 2
+    n = FRAMES * HID
+    win_ref[rows * BLOCK : rows * BLOCK + 16, :] = jnp.zeros((16, COLS), BF16)
+    filled = 0
+    for step in range(hidden_rows + LAG2 + LAG3):
+        want = min(rows, step + 3 + AHEAD)
+        while 2 * filled < want:
+            fill_pair(flags, refs, win_ref, filled, level)
+            filled += 1
+        if step < hidden_rows:
+            start = step * BLOCK
+            half = jnp.dot(w1_ref[...], win_ref[start : start + DEPTH, :], preferred_element_type=F32)
+            hid_ref[step * n : (step + 1) * n, :] = (half + half * jnp.tanh(half)).astype(BF16)
+        row = step - LAG2
+        if 0 <= row < hidden_rows:
+            prod_ref[row * 72 : (row + 1) * 72, :] = jnp.dot(
+                w2_ref[...], hid_ref[row * n : (row + 1) * n, :], preferred_element_type=F32
             )
-            win_ref[(row + sub) * BLOCK : (row + sub + 1) * BLOCK, :] = block.astype(BF16)
-    win_ref[rows * BLOCK : rows * BLOCK + 16, :] = jnp.zeros((16, COLS), BF16)
-
-
-def hidden_products(w1_ref, w2_ref, win_ref, prod_ref, hidden_rows):
-    def one_row(row, carry):
-        start = pl.multiple_of(row * BLOCK, 16)
-        half = jnp.dot(w1_ref[...], win_ref[pl.ds(start, DEPTH), :], preferred_element_type=F32)
-        hidden = (half + half * jnp.tanh(half)).astype(BF16)
-        out = jnp.dot(w2_ref[...], hidden, preferred_element_type=F32)
-        prod_ref[pl.ds(pl.multiple_of(row * 72, 8), 72), :] = out
-        return carry
-
-    lax.fori_loop(0, hidden_rows, one_row, 0, unroll=2)
+        row = step - LAG2 - LAG3
+        if row >= 2:
+            emit(row - 2)
 
 
 def net_row(prod_ref, row):
@@ -202,49 +210,46 @@
 
 def first_kernel(
     flags_ref, x_in, noise_in, up_ref, down_ref, core_ref, own_ref, far_ref, w1_ref, w2_ref,
-    count_ref, total_ref, next_ref, send_ref, win_ref, prod_ref, x_ref, noise_ref,
+    count_ref, total_ref, next_ref, send_ref, win_ref, hid_ref, prod_ref, x_ref, noise_ref,
 ):
-    rows = 2 * ROWS
     split_halves(x_in, x_ref)
     split_halves(noise_in, noise_ref)
-    fill_windows(flags_ref, core_ref, own_ref, far_ref, win_ref, rows, LEVELS[0])
-    hidden_products(w1_ref, w2_ref, win_ref, prod_ref, rows - 2)
     grow = (1.0 + LEVELS[0] ** 2) ** 0.5
     shrink = 1.0 / (1.0 + LEVELS[1] ** 2) ** 0.5
-    for row in range(0, ROWS + 4, 2):
-        both = []
-        if row == 0:
-            x_pair = up_ref[(ROWS - 2) * FL : ROWS * FL, :].astype(F32) * grow
-            noise_pair = up_ref[MSG_NOISE + 2 * FL : MSG_NOISE + 4 * FL, :].astype(F32)
-        elif row == ROWS + 2:
-            x_pair = down_ref[0 : 2 * FL, :].astype(F32) * grow
-            noise_pair = down_ref[MSG_NOISE : MSG_NOISE + 2 * FL, :].astype(F32)
-        for sub in range(2):
-            part = slice(sub * FL, (sub + 1) * FL)
-            here = row + sub
-            inside = 2 <= here < ROWS + 2
-            x = row_of(x_ref, here - 2) if inside else x_pair[part]
-            noise = row_of(noise_ref, here - 2) if inside else noise_pair[part]
-            at = slice(here * FL, (here + 1) * FL)
-            new = advance(
-                x, noise, net_row(prod_ref, here), count_ref[at, :], total_ref[at, :], 0
-            )
-            if inside:
-                next_ref[(here - 2) * FL : (here - 1) * FL, :] = new
-            both.append(new)
-        pair = jnp.concatenate(both, axis=0) * shrink
-        send_ref[row * FL : (row + 2) * FL, :] = pair.astype(BF16)
+    made = {}
+
+    def emit(here):
+        part = slice((here % 2) * FL, (here % 2 + 1) * FL)
+        if here < 2:
+            x = up_ref[(ROWS - 2) * FL : ROWS * FL, :].astype(F32)[part] * grow
+            noise = up_ref[MSG_NOISE + 2 * FL : MSG_NOISE + 4 * FL, :].astype(F32)[part]
+        elif here >= ROWS + 2:
+            x = down_ref[0 : 2 * FL, :].astype(F32)[part] * grow
+            noise = down_ref[MSG_NOISE : MSG_NOISE + 2 * FL, :].astype(F32)[part]
+        else:
+            x, noise = row_of(x_ref, here - 2), row_of(noise_ref, here - 2)
+        at = slice(here * FL, (here + 1) * FL)
+        new = advance(x, noise, net_row(prod_ref, here), count_ref[at, :], total_ref[at, :], 0)
+        if 2 <= here < ROWS + 2:
+            next_ref[(here - 2) * FL : (here - 1) * FL, :] = new
+        made[here % 2] = new
+        if here % 2:
+            pair = jnp.concatenate([made[0], made[1]], axis=0) * shrink
+            send_ref[(here - 1) * FL : (here + 1) * FL, :] = pair.astype(BF16)
+
+    run_rows(
+        flags_ref, (core_ref, own_ref, far_ref), w1_ref, w2_ref, win_ref, hid_ref, prod_ref,
+        2 * ROWS, LEVELS[0], emit,
+    )
 
 
 def second_kernel(
     flags_ref, x_ref, noise_in, core_ref, own_ref, far_ref, w1_ref, w2_ref,
-    count_ref, total_ref, out_ref, win_ref, prod_ref, noise_ref, half_ref,
+    count_ref, total_ref, out_ref, win_ref, hid_ref, prod_ref, noise_ref, half_ref,
 ):
-    rows = ROWS + 4
     split_halves(noise_in, noise_ref)
-    fill_windows(flags_ref, core_ref, own_ref, far_ref, win_ref, rows, LEVELS[1])
-    hidden_products(w1_ref, w2_ref, win_ref, prod_ref, rows - 2)
-    for row in range(ROWS):
+
+    def emit(row):
         at = slice((row + 2) * FL, (row + 3) * FL)
         new = advance(
             x_ref[row * FL : (row + 1) * FL, :], row_of(noise_ref, row), net_row(prod_ref, row),
@@ -252,6 +257,11 @@
         )
         half_ref[pl.ds(row, FL, stride=ROWS), :] = new[:, 0:128]
         half_ref[pl.ds(ROWS * FL + row, FL, stride=ROWS), :] = new[:, 128:256]
+
+    run_rows(
+        flags_ref, (core_ref, own_ref, far_ref), w1_ref, w2_ref, win_ref, hid_ref, prod_ref,
+        ROWS + 4, LEVELS[1], emit,
+    )
     out_ref[:, 0:128] = half_ref[0 : ROWS * FL, :]
     out_ref[:, 128:256] = half_ref[ROWS * FL :, :]
 
@@ -290,6 +300,43 @@
         lax.ppermute(block, ("tm", "rows"), core),
         lax.ppermute(block, ("tm", "rows"), far),
     )
+
+
+def scratch_for(rows):
+    halves = pltpu.VMEM((2 * ROWS * FL, 128), F32)
+    return [
+        pltpu.VMEM((rows * BLOCK + 16, COLS), BF16),
+        pltpu.VMEM(((rows - 2) * FRAMES * HID, COLS), BF16),
+        pltpu.VMEM(((rows - 2) * 72, COLS), F32),
+        halves,
+        halves,
+    ]
+
+
+def first_call(*args):
+    shape = jax.ShapeDtypeStruct
+    return call(
+        first_kernel,
+        args,
+        [SMEM] + [VMEM] * 11,
+        [shape((ROWS * FL, COLS), F32), shape(((ROWS + 4) * FL, COLS), BF16)],
+        scratch_for(2 * ROWS),
+        name="first",
+        flops=14 * 2 * 256 * 384 * (256 + 72),
+    )
+
+
+def second_call(*args):
+    (out,) = call(
+        second_kernel,
+        args,
+        [SMEM] + [VMEM] * 9,
+        [jax.ShapeDtypeStruct((FL * ROWS, COLS), F32)],
+        scratch_for(ROWS + 4),
+        name="second",
+        flops=10 * 2 * 256 * 384 * (256 + 72),
+    )
+    return out
 
 
 def per_device(
@@ -313,10 +360,11 @@
         ]
     )
 
+    scaled = (x / (1.0 + LEVELS[0] ** 2) ** 0.5).astype(BF16)
     halves = pltpu.VMEM((2 * ROWS * FL, 128), F32)
     (msg,) = call(
         pack_kernel,
-        (obs_count, x, noise_a, line(obs_step), line(obs_row), line(obs_col), line(obs_value)),
+        (obs_count, scaled, noise_a, line(obs_step), line(obs_row), line(obs_col), line(obs_value)),
         [SMEM] + [VMEM] * 6,
         [shape((MSG_ROWS, COLS), BF16)],
         [halves, halves],
@@ -340,31 +388,11 @@
     core, far = exchange_time(own, n_tm, n_rows)
     maps = shape(((ROWS + 4) * FL, COLS), F32)
     count, total = call(maps_kernel, (msg, up, down), [VMEM] * 3, [maps, maps], name="maps")
-    scratch = lambda n: [
-        pltpu.VMEM((n * BLOCK + 16, COLS), BF16),
-        pltpu.VMEM(((n - 2) * 72, COLS), F32),
-        halves,
-        halves,
-    ]
-    current, send = call(
-        first_kernel,
-        (flags, x, noise_a, up, down, core, own, far, w1, w2, count, total),
-        [SMEM] + [VMEM] * 11,
-        [shape((ROWS * FL, COLS), F32), shape(((ROWS + 4) * FL, COLS), BF16)],
-        scratch(2 * ROWS),
-        name="first",
-        flops=14 * 2 * 256 * 384 * (256 + 72),
+    current, send = first_call(
+        flags, x, noise_a, up, down, core, own, far, w1, w2, count, total
     )
     core, far = exchange_time(send, n_tm, n_rows)
-    (out,) = call(
-        second_kernel,
-        (flags, current, noise_b, core, send, far, w1, w2, count, total),
-        [SMEM] + [VMEM] * 9,
-        [shape((FL * ROWS, COLS), F32)],
-        scratch(ROWS + 4),
-        name="second",
-        flops=10 * 2 * 256 * 384 * (256 + 72),
-    )
+    out = second_call(flags, current, noise_b, core, send, far, w1, w2, count, total)
     return out.reshape(noisy_states.shape)
 
 

time: 27.9 us -> 21.2 us (0.76)
  Pallas kernels: 11 us -> 5.14 us
  local copies, waits for them, and re-layouts: 3.72 us -> 2.04 us
  other arithmetic: 0.08 us -> 0.93 us
    pallas_call x5, Pallas kernels: 11 us -> 5.14 us  [call(): pl.pallas_call(kernel, out_shape=tuple(outs), in_specs=specs, out_specs=t...]
    unnamed x25 -> x21, local copies, waits for them, and re-layouts: 3.72 us -> 2.03 us
    convert_element_type x0 -> x1, other arithmetic: none -> 0.85 us  [per_device(): scaled = (x / (1.0 + LEVELS[0] ** 2) ** 0.5).astype(BF16)]
  transfers between devices with their start and end apart: 5 -> 5, of which waited for: 3 -> 3; matrix products, arithmetic and copies ran while one was open for 1% -> 1% of each run, Pallas kernels for 2% -> 3%
where the time goes in v2:
time: 21.2 us; the launch traced here: 21 us
  waiting for transfers between devices  7.18 us (34%)
  Pallas kernels  5.14 us (24%)
  starting transfers between devices  4.91 us (23%)
  local copies, waits for them, and re-layouts  2.04 us (10%)
  other arithmetic  0.93 us (4%)
  between operations  0.78 us (4%)
    ppermute x2, waiting for transfers between devices, exchange_time(): lax.ppermute(block, ('tm', 'rows'), far)  6.07 us
    pallas_call x5, Pallas kernels, call(): pl.pallas_call(kernel, out_shape=tuple(outs), in_specs=specs, out_specs=t...  5.14 us
    ppermute x2, starting transfers between devices, exchange_time(): lax.ppermute(block, ('tm', 'rows'), far)  2.63 us
    unnamed x21, local copies, waits for them, and re-layouts  2.03 us
    ppermute x2, starting transfers between devices, exchange_time(): lax.ppermute(block, ('tm', 'rows'), core)  1.96 us
    ppermute x1, waiting for transfers between devices, per_device(): lax.ppermute(msg, 'rows', [(i, (i + 1) % n_rows) for i in range(n_rows)])  1.1 us
    convert_element_type x1, other arithmetic, per_device(): scaled = (x / (1.0 + LEVELS[0] ** 2) ** 0.5).astype(BF16)  0.85 us
  transfers between devices with their start and end apart: 5, of which 3 were waited for; matrix products, arithmetic and copies ran while one was open for 1% of the time, Pallas kernels for 3%

profile of v2, /device:TPU:15, one launch (start us, length us, event | category | flops | bytes accessed | tf_op | source)
XLA Modules:
  0.0 21.0 jit_solution(2135481255673475989)
XLA Ops:
  0.0 0.0 copy-start.1
  0.7 0.8 %multiply_convert_fusion.scaled_in = bf16[64,256]{1,0:T(8,128)(2,1)S(1)} fusion(f32[4,2,8,256]{3,2,1,0:T(8,128)} %param.11), kind=kLoop, calls=%fused_computation.1 | loop fusion | flops 32768 | bytes 98304 | tf_op jit(solution)/shard_map/convert_element_type | solution.py:363
  1.5 0.0 copy-start.6
  1.5 0.0 copy-start.4
  1.6 0.0 copy-start.5
  1.6 0.0 copy-start.3
  1.6 0.0 copy-done.1
  1.6 0.6 %copy-done.6 = f32[1,1,256]{2,1,0:T(1,128)S(1)} copy-done((f32[1,1,256]{2,1,0:T(1,128)S(1)}, f32[1,1,256]{2,1,0:T(1,128)}, u32[]{:S(2)}) %copy-start.6) | copy-done | bytes 1048
  2.2 0.0 copy-done.4
  2.2 0.0 copy-done.5
  2.2 0.0 copy-done.3
  2.3 0.0 copy-start.9
  2.3 0.3 %collective-permute-start = (bf16[112,256]{1,0:T(8,128)(2,1)S(1)}, bf16[112,256]{1,0:T(8,128)(2,1)S(1)}, u32[]{:S(2)}, u32[]{:S(2)}) collective-permute-start(bf16[112,256]{1,0:T(8,128)(2,1)S(1)} %pack.1.msg_ref), channel_id=1, source_target_pairs={{0,1},{1,0},{2,3},{3,2},{4,5},{5,4},{6,7},{7,6},{8,9},{9,8},{10,11... | collective-permute-start | bytes 172040 | tf_op jit(solution)/shard_map/ppermute | solution.py:373
  2.6 0.5 %copy-done.9 = bf16[9,96,18]{1,2,0:T(8,128)(2,1)S(1)} copy-done((bf16[9,96,18]{1,2,0:T(8,128)(2,1)S(1)}, bf16[9,96,18]{1,2,0:T(8,128)(2,1)}, u32[]{:S(2)}) %copy-start.9) | copy-done | bytes 31128
  3.1 0.0 copy-start.2
  3.1 0.2 copy.12.conv_in_ref
  3.3 0.0 copy-start.7
  3.3 0.5 %copy-done.2 = bf16[9,2,96]{2,1,0:T(2,128)(2,1)S(1)} copy-done((bf16[9,2,96]{2,1,0:T(2,128)(2,1)S(1)}, bf16[9,2,96]{2,1,0:T(2,128)(2,1)}, u32[]{:S(2)}) %copy-start.2) | copy-done | bytes 3480
  3.8 0.2 copy-done.7
  4.0 0.3 %weights.1 = (bf16[384,256]{1,0:T(8,128)(2,1)S(1)}, bf16[72,384]{1,0:T(8,128)(2,1)S(1)}) custom-call(bf16[9,96,18]{2,1,0:T(8,128)(2,1)S(1)} %copy.12.conv_in_ref, bf16[9,2,96]{2,1,0:T(2,128)(2,1)S(1)} %copy-done.2, f32[1,96]{1,0:T(1,128)S(1)} %bitcast.20), custom_call_target="tpu_custom_call" | custom-call | bytes 286848 | tf_op jit(solution)/shard_map/weights/pallas_call | solution.py:272
  4.3 1.1 %collective-permute-done.up_ref.down_ref = bf16[112,256]{1,0:T(8,128)(2,1)S(1)} collective-permute-done((bf16[112,256]{1,0:T(8,128)(2,1)S(1)}, bf16[112,256]{1,0:T(8,128)(2,1)S(1)}, u32[]{:S(2)}, u32[]{:S(2)}) %collective-permute-start) | collective-permute-done | bytes 57376 | tf_op jit(solution)/shard_map/ppermute | solution.py:373
  5.4 1.9 %collective-permute-start.1 = (bf16[128,256]{1,0:T(8,128)(2,1)S(1)}, bf16[128,256]{1,0:T(8,128)(2,1)S(1)}, u32[]{:S(2)}, u32[]{:S(2)}) collective-permute-start(bf16[128,256]{1,0:T(8,128)(2,1)S(1)} %pad_maximum_fusion.own_ref), channel_id=1, source_target_pairs={{0,2},{2,0},{4,6},{6,4},{8,10},{10,8},{12,14},{14,12},{16,18},{18,... | collective-permute-start | bytes 196616 | tf_op jit(solution)/shard_map/ppermute | solution.py:300
  7.3 1.2 %collective-permute-start.2 = (bf16[128,256]{1,0:T(8,128)(2,1)S(1)}, bf16[128,256]{1,0:T(8,128)(2,1)S(1)}, u32[]{:S(2)}, u32[]{:S(2)}) collective-permute-start(bf16[128,256]{1,0:T(8,128)(2,1)S(1)} %pad_maximum_fusion.own_ref), channel_id=1, source_target_pairs={{2,4},{4,2},{6,8},{8,6},{10,12},{12,10},{14,16},{16,14},{18,20},{2... | collective-permute-start | bytes 196616 | tf_op jit(solution)/shard_map/ppermute | solution.py:301
  8.5 0.1 add_convert_fusion.flags_ref
  8.6 0.0 copy-start
  8.6 0.3 %maps.1 = (f32[96,256]{1,0:T(8,128)S(1)}, f32[96,256]{1,0:T(8,128)S(1)}) custom-call(bf16[112,256]{1,0:T(8,128)(2,1)S(1)} %pack.1.msg_ref, bf16[112,256]{1,0:T(8,128)(2,1)S(1)} %collective-permute-done.up_ref.down_ref, bf16[112,256]{1,0:T(8,128)(2,1)S(1)} %collective-permute-done.up_ref.down_ref), custom_call_target="tpu_custom_call" | custom-call | bytes 368640 | tf_op jit(solution)/shard_map/maps/pallas_call | solution.py:272
  8.9 0.0 collective-permute-done.1.core_ref
  8.9 3.0 %collective-permute-done.2.far_ref = bf16[128,256]{1,0:T(8,128)(2,1)S(1)} collective-permute-done((bf16[128,256]{1,0:T(8,128)(2,1)S(1)}, bf16[128,256]{1,0:T(8,128)(2,1)S(1)}, u32[]{:S(2)}, u32[]{:S(2)}) %collective-permute-start.2) | collective-permute-done | bytes 65568 | tf_op jit(solution)/shard_map/ppermute | solution.py:301
  11.9 0.0 copy-done
  11.9 0.0 copy-start.8
  11.9 2.1 %first.1 = (f32[64,256]{1,0:T(8,128)S(1)}, bf16[96,256]{1,0:T(8,128)(2,1)S(1)}) custom-call(s32[3]{0:T(128)S(1)} %add_convert_fusion.flags_ref, f32[64,256]{1,0:T(8,128)S(1)} %bitcast.13, f32[64,256]{1,0:T(8,128)S(1)} %bitcast.15, bf16[112,256]{1,0:T(8,128)(2,1)S(1)} %collective-permute-done.up_ref.down_ref, ...), custom_call_target="tpu_custom_call" | custom-call | flops 902823936 | bytes 1005580 | tf_op jit(solution)/shard_map/first/pallas_call | solution.py:272
  14.0 0.1 collective-permute-start.3
  14.1 1.4 %collective-permute-start.4 = (bf16[96,256]{1,0:T(8,128)(2,1)S(1)}, bf16[96,256]{1,0:T(8,128)(2,1)S(1)}, u32[]{:S(2)}, u32[]{:S(2)}) collective-permute-start(bf16[96,256]{1,0:T(8,128)(2,1)S(1)} %get-tuple-element.16.own_ref), channel_id=1, source_target_pairs={{2,4},{4,2},{6,8},{8,6},{10,12},{12,10},{14,16},{16,14},{18,20},{2... | collective-permute-start | bytes 147464 | tf_op jit(solution)/shard_map/ppermute | solution.py:301
  15.5 0.0 collective-permute-done.3.core_ref
  15.5 3.1 %collective-permute-done.4.far_ref = bf16[96,256]{1,0:T(8,128)(2,1)S(1)} collective-permute-done((bf16[96,256]{1,0:T(8,128)(2,1)S(1)}, bf16[96,256]{1,0:T(8,128)(2,1)S(1)}, u32[]{:S(2)}, u32[]{:S(2)}) %collective-permute-start.4) | collective-permute-done | bytes 49184 | tf_op jit(solution)/shard_map/ppermute | solution.py:301
  18.6 0.0 copy-done.8
  18.6 2.4 %second.1 = f32[64,256]{1,0:T(8,128)} custom-call(s32[3]{0:T(128)S(1)} %add_convert_fusion.flags_ref, f32[64,256]{1,0:T(8,128)S(1)} %get-tuple-element.15.x_ref, f32[64,256]{1,0:T(8,128)S(1)} %bitcast.21, bf16[96,256]{1,0:T(8,128)(2,1)S(1)} %collective-permute-done.3.core_ref, bf16[96,256]{1,0:T(8,128)(2,1)S(1)} %get-tuple-element.16.own_ref, ...), custom_call_target="tpu_custom_call" | custom-call | flops 644874240 | bytes 792588 | tf_op jit(solution)/shard_map/second/pallas_call | solution.py:272
  (4 shorter events, 0.1 us)
Async XLA Ops:
  0.0 1.6 %copy-start.1 = (f32[4,2,8,256]{3,2,1,0:T(8,128)S(1)}, f32[4,2,8,256]{3,2,1,0:T(8,128)}, u32[]{:S(2)}) copy-start(f32[4,2,8,256]{3,2,1,0:T(8,128)} %param.12) | copy-start | bytes 196612
  1.5 0.7 %copy-start.6 = (f32[1,1,256]{2,1,0:T(1,128)S(1)}, f32[1,1,256]{2,1,0:T(1,128)}, u32[]{:S(2)}) copy-start(f32[1,1,256]{2,1,0:T(1,128)} %param.21) | copy-start | bytes 3076
  1.5 0.7 %copy-start.4 = (s32[1,1,256]{2,1,0:T(1,128)S(1)}, s32[1,1,256]{2,1,0:T(1,128)}, u32[]{:S(2)}) copy-start(s32[1,1,256]{2,1,0:T(1,128)} %param.19) | copy-start | bytes 3076
  1.6 0.7 %copy-start.5 = (s32[1,1,256]{2,1,0:T(1,128)S(1)}, s32[1,1,256]{2,1,0:T(1,128)}, u32[]{:S(2)}) copy-start(s32[1,1,256]{2,1,0:T(1,128)} %param.20) | copy-start | bytes 3076
  1.6 0.7 %copy-start.3 = (s32[1,1,256]{2,1,0:T(1,128)S(1)}, s32[1,1,256]{2,1,0:T(1,128)}, u32[]{:S(2)}) copy-start(s32[1,1,256]{2,1,0:T(1,128)} %param.18) | copy-start | bytes 3076
  2.3 0.8 %copy-start.9 = (bf16[9,96,18]{1,2,0:T(8,128)(2,1)S(1)}, bf16[9,96,18]{1,2,0:T(8,128)(2,1)}, u32[]{:S(2)}) copy-start(bf16[9,96,18]{1,2,0:T(8,128)(2,1)} %param.14) | copy-start | bytes 93316
  2.3 3.1 %collective-permute-start = (bf16[112,256]{1,0:T(8,128)(2,1)S(1)}, bf16[112,256]{1,0:T(8,128)(2,1)S(1)}, u32[]{:S(2)}, u32[]{:S(2)}) collective-permute-start(bf16[112,256]{1,0:T(8,128)(2,1)S(1)} %pack.1.msg_ref), channel_id=1, source_target_pairs={{0,1},{1,0},{2,3},{3,2},{4,5},{5,4},{6,7},{7,6},{8,9},{9,8},{10,11... | collective-permute-start | bytes 172040 | tf_op jit(solution)/shard_map/ppermute | solution.py:373
  3.1 0.7 %copy-start.2 = (bf16[9,2,96]{2,1,0:T(2,128)(2,1)S(1)}, bf16[9,2,96]{2,1,0:T(2,128)(2,1)}, u32[]{:S(2)}) copy-start(bf16[9,2,96]{2,1,0:T(2,128)(2,1)} %conv_out_ref.1) | copy-start | bytes 10372
  3.3 0.7 %copy-start.7 = (f32[96]{0:T(128)S(1)}, f32[96]{0:T(128)}, u32[]{:S(2)}) copy-start(f32[96]{0:T(128)} %param.16) | copy-start | bytes 1156
  5.4 3.4 %collective-permute-start.1 = (bf16[128,256]{1,0:T(8,128)(2,1)S(1)}, bf16[128,256]{1,0:T(8,128)(2,1)S(1)}, u32[]{:S(2)}, u32[]{:S(2)}) collective-permute-start(bf16[128,256]{1,0:T(8,128)(2,1)S(1)} %pad_maximum_fusion.own_ref), channel_id=1, source_target_pairs={{0,2},{2,0},{4,6},{6,4},{8,10},{10,8},{12,14},{14,12},{16,18},{18,... | collective-permute-start | bytes 196616 | tf_op jit(solution)/shard_map/ppermute | solution.py:300
  7.3 4.6 %collective-permute-start.2 = (bf16[128,256]{1,0:T(8,128)(2,1)S(1)}, bf16[128,256]{1,0:T(8,128)(2,1)S(1)}, u32[]{:S(2)}, u32[]{:S(2)}) collective-permute-start(bf16[128,256]{1,0:T(8,128)(2,1)S(1)} %pad_maximum_fusion.own_ref), channel_id=1, source_target_pairs={{2,4},{4,2},{6,8},{8,6},{10,12},{12,10},{14,16},{16,14},{18,20},{2... | collective-permute-start | bytes 196616 | tf_op jit(solution)/shard_map/ppermute | solution.py:301
  8.6 3.3 %copy-start = (f32[4,2,8,256]{3,2,1,0:T(8,128)S(1)}, f32[4,2,8,256]{3,2,1,0:T(8,128)}, u32[]{:S(2)}) copy-start(f32[4,2,8,256]{3,2,1,0:T(8,128)} %param.11) | copy-start | bytes 196612
  11.9 6.7 %copy-start.8 = (f32[4,2,8,256]{3,2,1,0:T(8,128)S(1)}, f32[4,2,8,256]{3,2,1,0:T(8,128)}, u32[]{:S(2)}) copy-start(f32[4,2,8,256]{3,2,1,0:T(8,128)} %param.13) | copy-start | bytes 196612
  14.0 1.5 %collective-permute-start.3 = (bf16[96,256]{1,0:T(8,128)(2,1)S(1)}, bf16[96,256]{1,0:T(8,128)(2,1)S(1)}, u32[]{:S(2)}, u32[]{:S(2)}) collective-permute-start(bf16[96,256]{1,0:T(8,128)(2,1)S(1)} %get-tuple-element.16.own_ref), channel_id=1, source_target_pairs={{0,2},{2,0},{4,6},{6,4},{8,10},{10,8},{12,14},{14,12},{16,18},{18,... | collective-permute-start | bytes 147464 | tf_op jit(solution)/shard_map/ppermute | solution.py:300
  14.1 4.5 %collective-permute-start.4 = (bf16[96,256]{1,0:T(8,128)(2,1)S(1)}, bf16[96,256]{1,0:T(8,128)(2,1)S(1)}, u32[]{:S(2)}, u32[]{:S(2)}) collective-permute-start(bf16[96,256]{1,0:T(8,128)(2,1)S(1)} %get-tuple-element.16.own_ref), channel_id=1, source_target_pairs={{2,4},{4,2},{6,8},{8,6},{10,12},{12,10},{14,16},{16,14},{18,20},{2... | collective-permute-start | bytes 147464 | tf_op jit(solution)/shard_map/ppermute | solution.py:301

commit v3 on v2

--- a/solution.py
+++ b/solution.py
@@ -19,9 +19,8 @@
 GROUP = 3 * FL
 BLOCK = 80
 DEPTH = 256
-MSG_NOISE = ROWS * FL
-MSG_OBS = MSG_NOISE + 4 * FL
-MSG_ROWS = MSG_OBS + 16
+AUX_OBS = 4 * FL
+AUX_ROWS = AUX_OBS + 16
 NO_CELL = 64.0
 AHEAD, LAG2, LAG3 = 4, 3, 3
 VMEM = pl.BlockSpec(memory_space=pltpu.VMEM)
@@ -49,17 +48,18 @@
     return jnp.concatenate([left, right], axis=1)
 
 
-def pack_kernel(
-    count_ref, scaled_in, noise_in, step_ref, row_ref, col_ref, val_ref, msg_ref, scaled_ref, noise_ref
-):
+def pack_kernel(scaled_in, msg_ref, scaled_ref):
     split_halves(scaled_in, scaled_ref)
-    split_halves(noise_in, noise_ref)
     for row in range(0, ROWS, 2):
         pair = jnp.concatenate([row_of(scaled_ref, row), row_of(scaled_ref, row + 1)], axis=0)
         msg_ref[row * FL : (row + 2) * FL, :] = pair.astype(BF16)
+
+
+def aux_kernel(count_ref, noise_in, step_ref, row_ref, col_ref, val_ref, aux_ref, noise_ref):
+    split_halves(noise_in, noise_ref)
     for at, row in enumerate((0, ROWS - 2)):
         pair = jnp.concatenate([row_of(noise_ref, row), row_of(noise_ref, row + 1)], axis=0)
-        msg_ref[MSG_NOISE + 2 * at * FL : MSG_NOISE + 2 * (at + 1) * FL, :] = pair.astype(BF16)
+        aux_ref[2 * at * FL : 2 * (at + 1) * FL, :] = pair.astype(BF16)
     live = iota((1, COLS), 1) < count_ref[0, 0]
     cell = (row_ref[...] * FL + step_ref[...] * 2).astype(F32)
     cell = jnp.where(live, cell, NO_CELL)
@@ -71,7 +71,7 @@
     table = jnp.zeros((16, COLS), F32)
     for at, line in enumerate((cell, col_ref[...].astype(F32), high, middle, low)):
         table = jnp.where(which == at, line, table)
-    msg_ref[MSG_OBS : MSG_OBS + 16, :] = table.astype(BF16)
+    aux_ref[AUX_OBS:AUX_ROWS, :] = table.astype(BF16)
 
 
 def weights_kernel(conv_in_ref, conv_out_ref, embed_ref, w1_ref, w2_ref, wide_ref):
@@ -133,7 +133,7 @@
 
 
 def maps_kernel(msg_ref, up_ref, down_ref, count_ref, total_ref):
-    obs = slice(MSG_OBS, MSG_OBS + 16)
+    obs = slice(AUX_OBS, AUX_ROWS)
     pieces = (
         (up_ref, (ROWS - 2) * FL, 2 * FL, 0),
         (msg_ref, 0, ROWS * FL, 2 * FL),
@@ -209,8 +209,8 @@
 
 
 def first_kernel(
-    flags_ref, x_in, noise_in, up_ref, down_ref, core_ref, own_ref, far_ref, w1_ref, w2_ref,
-    count_ref, total_ref, next_ref, send_ref, win_ref, hid_ref, prod_ref, x_ref, noise_ref,
+    flags_ref, x_in, noise_in, aux_up_ref, aux_down_ref, core_ref, own_ref, far_ref, w1_ref,
+    w2_ref, count_ref, total_ref, next_ref, send_ref, win_ref, hid_ref, prod_ref, x_ref, noise_ref,
 ):
     split_halves(x_in, x_ref)
     split_halves(noise_in, noise_ref)
@@ -220,12 +220,11 @@
 
     def emit(here):
         part = slice((here % 2) * FL, (here % 2 + 1) * FL)
-        if here < 2:
-            x = up_ref[(ROWS - 2) * FL : ROWS * FL, :].astype(F32)[part] * grow
-            noise = up_ref[MSG_NOISE + 2 * FL : MSG_NOISE + 4 * FL, :].astype(F32)[part]
-        elif here >= ROWS + 2:
-            x = down_ref[0 : 2 * FL, :].astype(F32)[part] * grow
-            noise = down_ref[MSG_NOISE : MSG_NOISE + 2 * FL, :].astype(F32)[part]
+        if not 2 <= here < ROWS + 2:
+            at = (here + 2) // 2 * 2 * FL
+            x = own_ref[at : at + 2 * FL, :].astype(F32)[part] * grow
+            ref, start = (aux_up_ref, 2 * FL) if here < 2 else (aux_down_ref, 0)
+            noise = ref[start : start + 2 * FL, :].astype(F32)[part]
         else:
             x, noise = row_of(x_ref, here - 2), row_of(noise_ref, here - 2)
         at = slice(here * FL, (here + 1) * FL)
@@ -292,6 +291,13 @@
         for i in (0, n_tm - 1):
             far.append((at(i, r), at(i, r ^ 1)))
     return core, far
+
+
+def exchange_rows(block, n_rows):
+    up = lax.ppermute(block, "rows", [(i, (i + 1) % n_rows) for i in range(n_rows)])
+    if n_rows == 2:
+        return up, up
+    return up, lax.ppermute(block, "rows", [((i + 1) % n_rows, i) for i in range(n_rows)])
 
 
 def exchange_time(block, n_tm, n_rows):
@@ -364,17 +370,22 @@
     halves = pltpu.VMEM((2 * ROWS * FL, 128), F32)
     (msg,) = call(
         pack_kernel,
-        (obs_count, scaled, noise_a, line(obs_step), line(obs_row), line(obs_col), line(obs_value)),
-        [SMEM] + [VMEM] * 6,
-        [shape((MSG_ROWS, COLS), BF16)],
-        [halves, halves],
+        (scaled,),
+        [VMEM],
+        [shape((ROWS * FL, COLS), BF16)],
+        [halves],
         name="pack",
     )
-    up = lax.ppermute(msg, "rows", [(i, (i + 1) % n_rows) for i in range(n_rows)])
-    if n_rows == 2:
-        down = up
-    else:
-        down = lax.ppermute(msg, "rows", [((i + 1) % n_rows, i) for i in range(n_rows)])
+    (aux,) = call(
+        aux_kernel,
+        (obs_count, noise_a, line(obs_step), line(obs_row), line(obs_col), line(obs_value)),
+        [SMEM] + [VMEM] * 5,
+        [shape((AUX_ROWS, COLS), BF16)],
+        [halves],
+        name="aux",
+    )
+    up, down = exchange_rows(msg, n_rows)
+    aux_up, aux_down = exchange_rows(aux, n_rows)
     w1, w2 = call(
         weights_kernel,
         (conv_in, conv_out, line(level_embed)),
@@ -384,12 +395,12 @@
         name="weights",
     )
     half = ROWS * FL // 2
-    own = jnp.concatenate([up[half : 2 * half], msg[: 2 * half], down[:half]], axis=0)
+    own = jnp.concatenate([up[half:], msg, down[:half]], axis=0)
     core, far = exchange_time(own, n_tm, n_rows)
     maps = shape(((ROWS + 4) * FL, COLS), F32)
-    count, total = call(maps_kernel, (msg, up, down), [VMEM] * 3, [maps, maps], name="maps")
+    count, total = call(maps_kernel, (aux, aux_up, aux_down), [VMEM] * 3, [maps, maps], name="maps")
     current, send = first_call(
-        flags, x, noise_a, up, down, core, own, far, w1, w2, count, total
+        flags, x, noise_a, aux_up, aux_down, core, own, far, w1, w2, count, total
     )
     core, far = exchange_time(send, n_tm, n_rows)
     out = second_call(flags, current, noise_b, core, send, far, w1, w2, count, total)

time: 21.2 us -> 19.6 us (0.925)
  waiting for transfers between devices: 7.18 us -> 4.87 us
  starting transfers between devices: 4.91 us -> 6 us
  local copies, waits for them, and re-layouts: 2.04 us -> 1.56 us
    ppermute x1 -> x2, starting transfers between devices: 0.32 us -> 1.6 us  [exchange_rows(): lax.ppermute(block, 'rows', [(i, (i + 1) % n_rows) for i in range(n_rows)])]
    ppermute x2, waiting for transfers between devices: 6.07 us -> 4.86 us  [exchange_time(): lax.ppermute(block, ('tm', 'rows'), far)]
    ppermute x1 -> x2, waiting for transfers between devices: 1.1 us -> 0.01 us  [exchange_rows(): lax.ppermute(block, 'rows', [(i, (i + 1) % n_rows) for i in range(n_rows)])]
    unnamed x21, local copies, waits for them, and re-layouts: 2.03 us -> 1.56 us
    pallas_call x5 -> x6, Pallas kernels: 5.14 us -> 5.16 us  [call(): pl.pallas_call(kernel, out_shape=tuple(outs), in_specs=specs, out_specs=t...]
  transfers between devices with their start and end apart: 5 -> 6, of which waited for: 3 -> 2; matrix products, arithmetic and copies ran while one was open for 1% -> 1% of each run, Pallas kernels for 3% -> 3%
where the time goes in v3:
time: 19.6 us; the launch traced here: 19.3 us
  starting transfers between devices  6 us (31%)
  Pallas kernels  5.16 us (26%)
  waiting for transfers between devices  4.87 us (25%)
  local copies, waits for them, and re-layouts  1.56 us (8%)
  other arithmetic  0.96 us (5%)
  between operations  0.77 us (4%)
    pallas_call x6, Pallas kernels, call(): pl.pallas_call(kernel, out_shape=tuple(outs), in_specs=specs, out_specs=t...  5.16 us
    ppermute x2, waiting for transfers between devices, exchange_time(): lax.ppermute(block, ('tm', 'rows'), far)  4.86 us
    ppermute x2, starting transfers between devices, exchange_time(): lax.ppermute(block, ('tm', 'rows'), far)  2.63 us
    ppermute x2, starting transfers between devices, exchange_time(): lax.ppermute(block, ('tm', 'rows'), core)  1.78 us
    ppermute x2, starting transfers between devices, exchange_rows(): lax.ppermute(block, 'rows', [(i, (i + 1) % n_rows) for i in range(n_rows)])  1.6 us
    unnamed x21, local copies, waits for them, and re-layouts  1.56 us
    convert_element_type x1, other arithmetic, per_device(): scaled = (x / (1.0 + LEVELS[0] ** 2) ** 0.5).astype(BF16)  0.88 us
  transfers between devices with their start and end apart: 6, of which 2 were waited for; matrix products, arithmetic and copies ran while one was open for 1% of the time, Pallas kernels for 3%

profile of v3, /device:TPU:15, one launch (start us, length us, event | category | flops | bytes accessed | tf_op | source)
XLA Modules:
  0.0 19.3 jit_solution(11770674880998882290)
XLA Ops:
  0.0 0.0 copy-start.1
  0.0 0.9 %multiply_convert_fusion.scaled_in = bf16[64,256]{1,0:T(8,128)(2,1)S(1)} fusion(f32[4,2,8,256]{3,2,1,0:T(8,128)} %param.11), kind=kLoop, calls=%fused_computation.1 | loop fusion | flops 32768 | bytes 98304 | tf_op jit(solution)/shard_map/convert_element_type | solution.py:369
  0.9 0.3 %collective-permute-start.1 = (bf16[64,256]{1,0:T(8,128)(2,1)S(1)}, bf16[64,256]{1,0:T(8,128)(2,1)S(1)}, u32[]{:S(2)}, u32[]{:S(2)}) collective-permute-start(bf16[64,256]{1,0:T(8,128)(2,1)S(1)} %pack.1), channel_id=1, source_target_pairs={{0,1},{1,0},{2,3},{3,2},{4,5},{5,4},{6,7},{7,6},{8,9},{9,8},{10,11... | collective-permute-start | bytes 98312 | tf_op jit(solution)/shard_map/ppermute | solution.py:297
  1.9 0.0 copy-start.6
  1.9 0.0 copy-start.4
  1.9 0.0 copy-start.5
  1.9 0.0 copy-start.3
  1.9 0.0 copy-done.1
  1.9 0.6 %copy-done.6 = f32[1,1,256]{2,1,0:T(1,128)S(1)} copy-done((f32[1,1,256]{2,1,0:T(1,128)S(1)}, f32[1,1,256]{2,1,0:T(1,128)}, u32[]{:S(2)}) %copy-start.6) | copy-done | bytes 1048
  2.6 0.0 copy-done.4
  2.6 0.0 copy-done.5
  2.6 0.0 copy-done.3
  2.6 1.3 %collective-permute-start = (bf16[48,256]{1,0:T(8,128)(2,1)S(1)}, bf16[48,256]{1,0:T(8,128)(2,1)S(1)}, u32[]{:S(2)}, u32[]{:S(2)}) collective-permute-start(bf16[48,256]{1,0:T(8,128)(2,1)S(1)} %aux.1.msg_ref), channel_id=1, source_target_pairs={{0,1},{1,0},{2,3},{3,2},{4,5},{5,4},{6,7},{7,6},{8,9},{9,8},{10,11... | collective-permute-start | bytes 73736 | tf_op jit(solution)/shard_map/ppermute | solution.py:297
  3.9 0.0 collective-permute-done.1
  3.9 0.0 copy-start.9
  3.9 1.7 %collective-permute-start.2 = (bf16[128,256]{1,0:T(8,128)(2,1)S(1)}, bf16[128,256]{1,0:T(8,128)(2,1)S(1)}, u32[]{:S(2)}, u32[]{:S(2)}) collective-permute-start(bf16[128,256]{1,0:T(8,128)(2,1)S(1)} %pad_maximum_fusion.own_ref), channel_id=1, source_target_pairs={{0,2},{2,0},{4,6},{6,4},{8,10},{10,8},{12,14},{14,12},{16,18},{18,... | collective-permute-start | bytes 196616 | tf_op jit(solution)/shard_map/ppermute | solution.py:306
  5.6 1.2 %collective-permute-start.3 = (bf16[128,256]{1,0:T(8,128)(2,1)S(1)}, bf16[128,256]{1,0:T(8,128)(2,1)S(1)}, u32[]{:S(2)}, u32[]{:S(2)}) collective-permute-start(bf16[128,256]{1,0:T(8,128)(2,1)S(1)} %pad_maximum_fusion.own_ref), channel_id=1, source_target_pairs={{2,4},{4,2},{6,8},{8,6},{10,12},{12,10},{14,16},{16,14},{18,20},{2... | collective-permute-start | bytes 196616 | tf_op jit(solution)/shard_map/ppermute | solution.py:307
  6.8 0.1 add_convert_fusion.flags_ref
  6.9 0.0 copy-done.9
  6.9 0.0 copy-start.2
  6.9 0.2 %copy.12.conv_in_ref = bf16[9,96,18]{2,1,0:T(8,128)(2,1)S(1)} copy(bf16[9,96,18]{1,2,0:T(8,128)(2,1)S(1)} %copy-done.9) | data formatting | bytes 62208 | tf_op args[3]
  7.1 0.0 copy-start.7
  7.1 0.5 %copy-done.2 = bf16[9,2,96]{2,1,0:T(2,128)(2,1)S(1)} copy-done((bf16[9,2,96]{2,1,0:T(2,128)(2,1)S(1)}, bf16[9,2,96]{2,1,0:T(2,128)(2,1)}, u32[]{:S(2)}) %copy-start.2) | copy-done | bytes 3480
  7.6 0.2 copy-done.7
  7.8 0.3 %weights.1 = (bf16[384,256]{1,0:T(8,128)(2,1)S(1)}, bf16[72,384]{1,0:T(8,128)(2,1)S(1)}) custom-call(bf16[9,96,18]{2,1,0:T(8,128)(2,1)S(1)} %copy.12.conv_in_ref, bf16[9,2,96]{2,1,0:T(2,128)(2,1)S(1)} %copy-done.2, f32[1,96]{1,0:T(1,128)S(1)} %bitcast.20), custom_call_target="tpu_custom_call" | custom-call | bytes 286848 | tf_op jit(solution)/shard_map/weights/pallas_call | solution.py:271
  8.1 0.0 copy-start
  8.1 0.0 collective-permute-done.up_ref.down_ref.aux_up_ref.aux_down_ref
  8.1 0.3 %maps.1 = (f32[96,256]{1,0:T(8,128)S(1)}, f32[96,256]{1,0:T(8,128)S(1)}) custom-call(bf16[48,256]{1,0:T(8,128)(2,1)S(1)} %aux.1.msg_ref, bf16[48,256]{1,0:T(8,128)(2,1)S(1)} %collective-permute-done.up_ref.down_ref.aux_up_ref.aux_down_ref, bf16[48,256]{1,0:T(8,128)(2,1)S(1)} %collective-permute-done.up_ref.down_ref.aux_up_ref.aux_down_ref), custom_call_target="tpu_custom_call" | custom-call | bytes 270336 | tf_op jit(solution)/shard_map/maps/pallas_call | solution.py:271
  8.4 0.0 collective-permute-done.2.core_ref
  8.4 1.8 %collective-permute-done.3.far_ref = bf16[128,256]{1,0:T(8,128)(2,1)S(1)} collective-permute-done((bf16[128,256]{1,0:T(8,128)(2,1)S(1)}, bf16[128,256]{1,0:T(8,128)(2,1)S(1)}, u32[]{:S(2)}, u32[]{:S(2)}) %collective-permute-start.3) | collective-permute-done | bytes 65568 | tf_op jit(solution)/shard_map/ppermute | solution.py:307
  10.2 0.0 copy-done
  10.2 0.0 copy-start.8
  10.2 2.1 %first.1 = (f32[64,256]{1,0:T(8,128)S(1)}, bf16[96,256]{1,0:T(8,128)(2,1)S(1)}) custom-call(s32[3]{0:T(128)S(1)} %add_convert_fusion.flags_ref, f32[64,256]{1,0:T(8,128)S(1)} %bitcast.13, f32[64,256]{1,0:T(8,128)S(1)} %bitcast.15, bf16[48,256]{1,0:T(8,128)(2,1)S(1)} %collective-permute-done.up_ref.down_ref.aux_up_ref.aux_down_ref, ...), custom_call_target="tpu_custom_call" | custom-call | flops 902823936 | bytes 940044 | tf_op jit(solution)/shard_map/first/pallas_call | solution.py:271
  12.4 0.1 collective-permute-start.4
  12.4 1.4 %collective-permute-start.5 = (bf16[96,256]{1,0:T(8,128)(2,1)S(1)}, bf16[96,256]{1,0:T(8,128)(2,1)S(1)}, u32[]{:S(2)}, u32[]{:S(2)}) collective-permute-start(bf16[96,256]{1,0:T(8,128)(2,1)S(1)} %get-tuple-element.16.own_ref), channel_id=1, source_target_pairs={{2,4},{4,2},{6,8},{8,6},{10,12},{12,10},{14,16},{16,14},{18,20},{2... | collective-permute-start | bytes 147464 | tf_op jit(solution)/shard_map/ppermute | solution.py:307
  13.9 0.0 collective-permute-done.4.core_ref
  13.9 3.0 %collective-permute-done.5.far_ref = bf16[96,256]{1,0:T(8,128)(2,1)S(1)} collective-permute-done((bf16[96,256]{1,0:T(8,128)(2,1)S(1)}, bf16[96,256]{1,0:T(8,128)(2,1)S(1)}, u32[]{:S(2)}, u32[]{:S(2)}) %collective-permute-start.5) | collective-permute-done | bytes 49184 | tf_op jit(solution)/shard_map/ppermute | solution.py:307
  16.9 0.0 copy-done.8
  16.9 2.4 %second.1 = f32[64,256]{1,0:T(8,128)} custom-call(s32[3]{0:T(128)S(1)} %add_convert_fusion.flags_ref, f32[64,256]{1,0:T(8,128)S(1)} %get-tuple-element.15.x_ref, f32[64,256]{1,0:T(8,128)S(1)} %bitcast.21, bf16[96,256]{1,0:T(8,128)(2,1)S(1)} %collective-permute-done.4.core_ref, bf16[96,256]{1,0:T(8,128)(2,1)S(1)} %get-tuple-element.16.own_ref, ...), custom_call_target="tpu_custom_call" | custom-call | flops 644874240 | bytes 792588 | tf_op jit(solution)/shard_map/second/pallas_call | solution.py:271
  (4 shorter events, 0.1 us)
Async XLA Ops:
  0.0 1.9 %copy-start.1 = (f32[4,2,8,256]{3,2,1,0:T(8,128)S(1)}, f32[4,2,8,256]{3,2,1,0:T(8,128)}, u32[]{:S(2)}) copy-start(f32[4,2,8,256]{3,2,1,0:T(8,128)} %param.12) | copy-start | bytes 196612
  0.9 3.0 %collective-permute-start.1 = (bf16[64,256]{1,0:T(8,128)(2,1)S(1)}, bf16[64,256]{1,0:T(8,128)(2,1)S(1)}, u32[]{:S(2)}, u32[]{:S(2)}) collective-permute-start(bf16[64,256]{1,0:T(8,128)(2,1)S(1)} %pack.1), channel_id=1, source_target_pairs={{0,1},{1,0},{2,3},{3,2},{4,5},{5,4},{6,7},{7,6},{8,9},{9,8},{10,11... | collective-permute-start | bytes 98312 | tf_op jit(solution)/shard_map/ppermute | solution.py:297
  1.9 0.7 %copy-start.6 = (f32[1,1,256]{2,1,0:T(1,128)S(1)}, f32[1,1,256]{2,1,0:T(1,128)}, u32[]{:S(2)}) copy-start(f32[1,1,256]{2,1,0:T(1,128)} %param.21) | copy-start | bytes 3076
  1.9 0.7 %copy-start.4 = (s32[1,1,256]{2,1,0:T(1,128)S(1)}, s32[1,1,256]{2,1,0:T(1,128)}, u32[]{:S(2)}) copy-start(s32[1,1,256]{2,1,0:T(1,128)} %param.19) | copy-start | bytes 3076
  1.9 0.7 %copy-start.5 = (s32[1,1,256]{2,1,0:T(1,128)S(1)}, s32[1,1,256]{2,1,0:T(1,128)}, u32[]{:S(2)}) copy-start(s32[1,1,256]{2,1,0:T(1,128)} %param.20) | copy-start | bytes 3076
  1.9 0.7 %copy-start.3 = (s32[1,1,256]{2,1,0:T(1,128)S(1)}, s32[1,1,256]{2,1,0:T(1,128)}, u32[]{:S(2)}) copy-start(s32[1,1,256]{2,1,0:T(1,128)} %param.18) | copy-start | bytes 3076
  2.6 5.5 %collective-permute-start = (bf16[48,256]{1,0:T(8,128)(2,1)S(1)}, bf16[48,256]{1,0:T(8,128)(2,1)S(1)}, u32[]{:S(2)}, u32[]{:S(2)}) collective-permute-start(bf16[48,256]{1,0:T(8,128)(2,1)S(1)} %aux.1.msg_ref), channel_id=1, source_target_pairs={{0,1},{1,0},{2,3},{3,2},{4,5},{5,4},{6,7},{7,6},{8,9},{9,8},{10,11... | collective-permute-start | bytes 73736 | tf_op jit(solution)/shard_map/ppermute | solution.py:297
  3.9 3.0 %copy-start.9 = (bf16[9,96,18]{1,2,0:T(8,128)(2,1)S(1)}, bf16[9,96,18]{1,2,0:T(8,128)(2,1)}, u32[]{:S(2)}) copy-start(bf16[9,96,18]{1,2,0:T(8,128)(2,1)} %param.14) | copy-start | bytes 93316
  3.9 4.5 %collective-permute-start.2 = (bf16[128,256]{1,0:T(8,128)(2,1)S(1)}, bf16[128,256]{1,0:T(8,128)(2,1)S(1)}, u32[]{:S(2)}, u32[]{:S(2)}) collective-permute-start(bf16[128,256]{1,0:T(8,128)(2,1)S(1)} %pad_maximum_fusion.own_ref), channel_id=1, source_target_pairs={{0,2},{2,0},{4,6},{6,4},{8,10},{10,8},{12,14},{14,12},{16,18},{18,... | collective-permute-start | bytes 196616 | tf_op jit(solution)/shard_map/ppermute | solution.py:306
  5.6 4.6 %collective-permute-start.3 = (bf16[128,256]{1,0:T(8,128)(2,1)S(1)}, bf16[128,256]{1,0:T(8,128)(2,1)S(1)}, u32[]{:S(2)}, u32[]{:S(2)}) collective-permute-start(bf16[128,256]{1,0:T(8,128)(2,1)S(1)} %pad_maximum_fusion.own_ref), channel_id=1, source_target_pairs={{2,4},{4,2},{6,8},{8,6},{10,12},{12,10},{14,16},{16,14},{18,20},{2... | collective-permute-start | bytes 196616 | tf_op jit(solution)/shard_map/ppermute | solution.py:307
  6.9 0.7 %copy-start.2 = (bf16[9,2,96]{2,1,0:T(2,128)(2,1)S(1)}, bf16[9,2,96]{2,1,0:T(2,128)(2,1)}, u32[]{:S(2)}) copy-start(bf16[9,2,96]{2,1,0:T(2,128)(2,1)} %conv_out_ref.1) | copy-start | bytes 10372
  7.1 0.7 %copy-start.7 = (f32[96]{0:T(128)S(1)}, f32[96]{0:T(128)}, u32[]{:S(2)}) copy-start(f32[96]{0:T(128)} %param.16) | copy-start | bytes 1156
  8.1 2.1 %copy-start = (f32[4,2,8,256]{3,2,1,0:T(8,128)S(1)}, f32[4,2,8,256]{3,2,1,0:T(8,128)}, u32[]{:S(2)}) copy-start(f32[4,2,8,256]{3,2,1,0:T(8,128)} %param.11) | copy-start | bytes 196612
  10.2 6.7 %copy-start.8 = (f32[4,2,8,256]{3,2,1,0:T(8,128)S(1)}, f32[4,2,8,256]{3,2,1,0:T(8,128)}, u32[]{:S(2)}) copy-start(f32[4,2,8,256]{3,2,1,0:T(8,128)} %param.13) | copy-start | bytes 196612
  12.4 1.5 %collective-permute-start.4 = (bf16[96,256]{1,0:T(8,128)(2,1)S(1)}, bf16[96,256]{1,0:T(8,128)(2,1)S(1)}, u32[]{:S(2)}, u32[]{:S(2)}) collective-permute-start(bf16[96,256]{1,0:T(8,128)(2,1)S(1)} %get-tuple-element.16.own_ref), channel_id=1, source_target_pairs={{0,2},{2,0},{4,6},{6,4},{8,10},{10,8},{12,14},{14,12},{16,18},{18,... | collective-permute-start | bytes 147464 | tf_op jit(solution)/shard_map/ppermute | solution.py:306
  12.4 4.5 %collective-permute-start.5 = (bf16[96,256]{1,0:T(8,128)(2,1)S(1)}, bf16[96,256]{1,0:T(8,128)(2,1)S(1)}, u32[]{:S(2)}, u32[]{:S(2)}) collective-permute-start(bf16[96,256]{1,0:T(8,128)(2,1)S(1)} %get-tuple-element.16.own_ref), channel_id=1, source_target_pairs={{2,4},{4,2},{6,8},{8,6},{10,12},{12,10},{14,16},{16,14},{18,20},{2... | collective-permute-start | bytes 147464 | tf_op jit(solution)/shard_map/ppermute | solution.py:307

commit v4 on v3

--- a/solution.py
+++ b/solution.py
@@ -1,11 +1,10 @@
-import functools
-
 import jax
 import jax.numpy as jnp
 from jax import lax
 from jax.experimental import pallas as pl
 from jax.experimental.pallas import tpu as pltpu
 from jax.sharding import PartitionSpec as P
+
 
 LEVELS = (1.0, 0.5, 0.2)
 OBS_NOISE = 0.1
@@ -60,7 +59,7 @@
     for at, row in enumerate((0, ROWS - 2)):
         pair = jnp.concatenate([row_of(noise_ref, row), row_of(noise_ref, row + 1)], axis=0)
         aux_ref[2 * at * FL : 2 * (at + 1) * FL, :] = pair.astype(BF16)
-    live = iota((1, COLS), 1) < count_ref[0, 0]
+    live = iota((1, COLS), 1) < count_ref[...]
     cell = (row_ref[...] * FL + step_ref[...] * 2).astype(F32)
     cell = jnp.where(live, cell, NO_CELL)
     val = val_ref[...]
@@ -265,7 +264,7 @@
     out_ref[:, 128:256] = half_ref[ROWS * FL :, :]
 
 
-def call(kernel, args, specs, outs, scratch=(), name=None, flops=0):
+def call(kernel, args, specs, outs, scratch=(), flops=0):
     moved = sum(a.size * a.dtype.itemsize for a in args)
     moved += sum(o.size * o.dtype.itemsize for o in outs)
     return pl.pallas_call(
@@ -276,7 +275,6 @@
         scratch_shapes=list(scratch),
         compiler_params=params(),
         cost_estimate=pl.CostEstimate(flops=flops, bytes_accessed=moved, transcendentals=0),
-        name=name,
     )(*args)
 
 
@@ -301,11 +299,10 @@
 
 
 def exchange_time(block, n_tm, n_rows):
-    core, far = time_pairs(n_tm, n_rows)
-    return (
-        lax.ppermute(block, ("tm", "rows"), core),
-        lax.ppermute(block, ("tm", "rows"), far),
-    )
+    core_pairs, far_pairs = time_pairs(n_tm, n_rows)
+    far = lax.ppermute(block, ("tm", "rows"), far_pairs)
+    core = lax.ppermute(block, ("tm", "rows"), core_pairs)
+    return core, far
 
 
 def scratch_for(rows):
@@ -327,7 +324,6 @@
         [SMEM] + [VMEM] * 11,
         [shape((ROWS * FL, COLS), F32), shape(((ROWS + 4) * FL, COLS), BF16)],
         scratch_for(2 * ROWS),
-        name="first",
         flops=14 * 2 * 256 * 384 * (256 + 72),
     )
 
@@ -339,7 +335,6 @@
         [SMEM] + [VMEM] * 9,
         [jax.ShapeDtypeStruct((FL * ROWS, COLS), F32)],
         scratch_for(ROWS + 4),
-        name="second",
         flops=10 * 2 * 256 * 384 * (256 + 72),
     )
     return out
@@ -368,21 +363,13 @@
 
     scaled = (x / (1.0 + LEVELS[0] ** 2) ** 0.5).astype(BF16)
     halves = pltpu.VMEM((2 * ROWS * FL, 128), F32)
-    (msg,) = call(
-        pack_kernel,
-        (scaled,),
-        [VMEM],
-        [shape((ROWS * FL, COLS), BF16)],
-        [halves],
-        name="pack",
-    )
+    (msg,) = call(pack_kernel, (scaled,), [VMEM], [shape((ROWS * FL, COLS), BF16)], [halves])
     (aux,) = call(
         aux_kernel,
         (obs_count, noise_a, line(obs_step), line(obs_row), line(obs_col), line(obs_value)),
-        [SMEM] + [VMEM] * 5,
+        [VMEM] * 6,
         [shape((AUX_ROWS, COLS), BF16)],
         [halves],
-        name="aux",
     )
     up, down = exchange_rows(msg, n_rows)
     aux_up, aux_down = exchange_rows(aux, n_rows)
@@ -392,13 +379,12 @@
         [VMEM] * 3,
         [shape((FRAMES * HID, DEPTH), BF16), shape((72, FRAMES * HID), BF16)],
         [pltpu.VMEM((HID, 128), F32)],
-        name="weights",
     )
     half = ROWS * FL // 2
     own = jnp.concatenate([up[half:], msg, down[:half]], axis=0)
     core, far = exchange_time(own, n_tm, n_rows)
     maps = shape(((ROWS + 4) * FL, COLS), F32)
-    count, total = call(maps_kernel, (aux, aux_up, aux_down), [VMEM] * 3, [maps, maps], name="maps")
+    count, total = call(maps_kernel, (aux, aux_up, aux_down), [VMEM] * 3, [maps, maps])
     current, send = first_call(
         flags, x, noise_a, aux_up, aux_down, core, own, far, w1, w2, count, total
     )

time: 19.6 us -> 19.6 us (level)
  no operation moved by 1% of the time
where the time goes in v4:
time: 19.6 us; the launch traced here: 19.3 us
  starting transfers between devices  5.94 us (30%)
  Pallas kernels  5.21 us (27%)
  waiting for transfers between devices  4.87 us (25%)
  local copies, waits for them, and re-layouts  1.56 us (8%)
  other arithmetic  0.96 us (5%)
  between operations  0.77 us (4%)
    pallas_call x6, Pallas kernels, call(): pl.pallas_call(kernel, out_shape=tuple(outs), in_specs=specs, out_specs=t...  5.21 us
    ppermute x2, waiting for transfers between devices, exchange_time(): far = lax.ppermute(block, ('tm', 'rows'), far_pairs)  4.86 us
    ppermute x2, starting transfers between devices, exchange_time(): far = lax.ppermute(block, ('tm', 'rows'), far_pairs)  2.63 us
    ppermute x2, starting transfers between devices, exchange_time(): core = lax.ppermute(block, ('tm', 'rows'), core_pairs)  1.77 us
    unnamed x21, local copies, waits for them, and re-layouts  1.56 us
    ppermute x2, starting transfers between devices, exchange_rows(): lax.ppermute(block, 'rows', [(i, (i + 1) % n_rows) for i in range(n_rows)])  1.54 us
    convert_element_type x1, other arithmetic, per_device(): scaled = (x / (1.0 + LEVELS[0] ** 2) ** 0.5).astype(BF16)  0.88 us
  transfers between devices with their start and end apart: 6, of which 2 were waited for; matrix products, arithmetic and copies ran while one was open for 1% of the time, Pallas kernels for 3%

profile of v4, /device:TPU:15, one launch (start us, length us, event | category | flops | bytes accessed | tf_op | source)
XLA Modules:
  0.0 19.3 jit_solution(6269313957491906714)
XLA Ops:
  0.0 0.0 copy-start.1
  0.0 0.9 %multiply_convert_fusion.scaled_in = bf16[64,256]{1,0:T(8,128)(2,1)S(1)} fusion(f32[4,2,8,256]{3,2,1,0:T(8,128)} %param.11), kind=kLoop, calls=%fused_computation.1 | loop fusion | flops 32768 | bytes 98304 | tf_op jit(solution)/shard_map/convert_element_type | solution.py:364
  0.9 0.3 %collective-permute-start.1 = (bf16[64,256]{1,0:T(8,128)(2,1)S(1)}, bf16[64,256]{1,0:T(8,128)(2,1)S(1)}, u32[]{:S(2)}, u32[]{:S(2)}) collective-permute-start(bf16[64,256]{1,0:T(8,128)(2,1)S(1)} %shard_map.110), channel_id=1, source_target_pairs={{0,1},{1,0},{2,3},{3,2},{4,5},{5,4},{6,7},{7,6},{8,9},{9,8},{10,11... | collective-permute-start | bytes 98312 | tf_op jit(solution)/shard_map/ppermute | solution.py:295
  1.9 0.0 copy-start.6
  1.9 0.0 copy-start.4
  1.9 0.0 copy-start.5
  1.9 0.0 copy-start.3
  1.9 0.0 copy-done.1
  1.9 0.6 %copy-done.6 = f32[1,1,256]{2,1,0:T(1,128)S(1)} copy-done((f32[1,1,256]{2,1,0:T(1,128)S(1)}, f32[1,1,256]{2,1,0:T(1,128)}, u32[]{:S(2)}) %copy-start.6) | copy-done | bytes 1048
  2.6 0.0 copy-done.4
  2.6 0.0 copy-done.5
  2.6 0.0 copy-done.3
  2.6 0.1 shard_map.109.msg_ref
  2.7 1.2 %collective-permute-start = (bf16[48,256]{1,0:T(8,128)(2,1)S(1)}, bf16[48,256]{1,0:T(8,128)(2,1)S(1)}, u32[]{:S(2)}, u32[]{:S(2)}) collective-permute-start(bf16[48,256]{1,0:T(8,128)(2,1)S(1)} %shard_map.109.msg_ref), channel_id=1, source_target_pairs={{0,1},{1,0},{2,3},{3,2},{4,5},{5,4},{6,7},{7,6},{8,9},{9,8},{10,11... | collective-permute-start | bytes 73736 | tf_op jit(solution)/shard_map/ppermute | solution.py:295
  3.9 0.0 collective-permute-done.1
  3.9 0.0 copy-start.9
  3.9 1.7 %collective-permute-start.2 = (bf16[128,256]{1,0:T(8,128)(2,1)S(1)}, bf16[128,256]{1,0:T(8,128)(2,1)S(1)}, u32[]{:S(2)}, u32[]{:S(2)}) collective-permute-start(bf16[128,256]{1,0:T(8,128)(2,1)S(1)} %pad_maximum_fusion.own_ref), channel_id=1, source_target_pairs={{0,2},{2,0},{4,6},{6,4},{8,10},{10,8},{12,14},{14,12},{16,18},{18,... | collective-permute-start | bytes 196616 | tf_op jit(solution)/shard_map/ppermute | solution.py:304
  5.6 1.2 %collective-permute-start.3 = (bf16[128,256]{1,0:T(8,128)(2,1)S(1)}, bf16[128,256]{1,0:T(8,128)(2,1)S(1)}, u32[]{:S(2)}, u32[]{:S(2)}) collective-permute-start(bf16[128,256]{1,0:T(8,128)(2,1)S(1)} %pad_maximum_fusion.own_ref), channel_id=1, source_target_pairs={{2,4},{4,2},{6,8},{8,6},{10,12},{12,10},{14,16},{16,14},{18,20},{2... | collective-permute-start | bytes 196616 | tf_op jit(solution)/shard_map/ppermute | solution.py:303
  6.8 0.1 add_convert_fusion.flags_ref
  6.9 0.0 copy-done.9
  6.9 0.0 copy-start.2
  6.9 0.2 %copy.12.conv_in_ref = bf16[9,96,18]{2,1,0:T(8,128)(2,1)S(1)} copy(bf16[9,96,18]{1,2,0:T(8,128)(2,1)S(1)} %copy-done.9) | data formatting | bytes 62208 | tf_op args[3]
  7.1 0.0 copy-start.7
  7.1 0.5 %copy-done.2 = bf16[9,2,96]{2,1,0:T(2,128)(2,1)S(1)} copy-done((bf16[9,2,96]{2,1,0:T(2,128)(2,1)S(1)}, bf16[9,2,96]{2,1,0:T(2,128)(2,1)}, u32[]{:S(2)}) %copy-start.2) | copy-done | bytes 3480
  7.6 0.2 copy-done.7
  7.8 0.3 %shard_map.111 = (bf16[384,256]{1,0:T(8,128)(2,1)S(1)}, bf16[72,384]{1,0:T(8,128)(2,1)S(1)}) custom-call(bf16[9,96,18]{2,1,0:T(8,128)(2,1)S(1)} %copy.12.conv_in_ref, bf16[9,2,96]{2,1,0:T(2,128)(2,1)S(1)} %copy-done.2, f32[1,96]{1,0:T(1,128)S(1)} %bitcast.20), custom_call_target="tpu_custom_call" | custom-call | bytes 286848 | tf_op jit(solution)/shard_map/pallas_call | solution.py:270
  8.1 0.0 copy-start
  8.1 0.0 collective-permute-done.up_ref.down_ref.aux_up_ref.aux_down_ref
  8.1 0.3 %shard_map.112 = (f32[96,256]{1,0:T(8,128)S(1)}, f32[96,256]{1,0:T(8,128)S(1)}) custom-call(bf16[48,256]{1,0:T(8,128)(2,1)S(1)} %shard_map.109.msg_ref, bf16[48,256]{1,0:T(8,128)(2,1)S(1)} %collective-permute-done.up_ref.down_ref.aux_up_ref.aux_down_ref, bf16[48,256]{1,0:T(8,128)(2,1)S(1)} %collective-permute-done.up_ref.down_ref.aux_up_ref.aux_down_ref), custom_call_target="tpu_custom_call" | custom-call | bytes 270336 | tf_op jit(solution)/shard_map/pallas_call | solution.py:270
  8.4 0.0 collective-permute-done.2.core_ref
  8.4 1.8 %collective-permute-done.3.far_ref = bf16[128,256]{1,0:T(8,128)(2,1)S(1)} collective-permute-done((bf16[128,256]{1,0:T(8,128)(2,1)S(1)}, bf16[128,256]{1,0:T(8,128)(2,1)S(1)}, u32[]{:S(2)}, u32[]{:S(2)}) %collective-permute-start.3) | collective-permute-done | bytes 65568 | tf_op jit(solution)/shard_map/ppermute | solution.py:303
  10.2 0.0 copy-done
  10.2 0.0 copy-start.8
  10.2 2.1 %shard_map.113 = (f32[64,256]{1,0:T(8,128)S(1)}, bf16[96,256]{1,0:T(8,128)(2,1)S(1)}) custom-call(s32[3]{0:T(128)S(1)} %add_convert_fusion.flags_ref, f32[64,256]{1,0:T(8,128)S(1)} %bitcast.13, f32[64,256]{1,0:T(8,128)S(1)} %bitcast.15, bf16[48,256]{1,0:T(8,128)(2,1)S(1)} %collective-permute-done.up_ref.down_ref.aux_up_ref.aux_down_ref, ...), custom_call_target="tpu_custom_call" | custom-call | flops 902823936 | bytes 940044 | tf_op jit(solution)/shard_map/pallas_call | solution.py:270
  12.4 0.1 collective-permute-start.4
  12.4 1.4 %collective-permute-start.5 = (bf16[96,256]{1,0:T(8,128)(2,1)S(1)}, bf16[96,256]{1,0:T(8,128)(2,1)S(1)}, u32[]{:S(2)}, u32[]{:S(2)}) collective-permute-start(bf16[96,256]{1,0:T(8,128)(2,1)S(1)} %get-tuple-element.16.own_ref), channel_id=1, source_target_pairs={{2,4},{4,2},{6,8},{8,6},{10,12},{12,10},{14,16},{16,14},{18,20},{2... | collective-permute-start | bytes 147464 | tf_op jit(solution)/shard_map/ppermute | solution.py:303
  13.9 0.0 collective-permute-done.4.core_ref
  13.9 3.0 %collective-permute-done.5.far_ref = bf16[96,256]{1,0:T(8,128)(2,1)S(1)} collective-permute-done((bf16[96,256]{1,0:T(8,128)(2,1)S(1)}, bf16[96,256]{1,0:T(8,128)(2,1)S(1)}, u32[]{:S(2)}, u32[]{:S(2)}) %collective-permute-start.5) | collective-permute-done | bytes 49184 | tf_op jit(solution)/shard_map/ppermute | solution.py:303
  16.9 0.0 copy-done.8
  16.9 2.4 %shard_map.114 = f32[64,256]{1,0:T(8,128)} custom-call(s32[3]{0:T(128)S(1)} %add_convert_fusion.flags_ref, f32[64,256]{1,0:T(8,128)S(1)} %get-tuple-element.15.x_ref, f32[64,256]{1,0:T(8,128)S(1)} %bitcast.21, bf16[96,256]{1,0:T(8,128)(2,1)S(1)} %collective-permute-done.4.core_ref, bf16[96,256]{1,0:T(8,128)(2,1)S(1)} %get-tuple-element.16.own_ref, ...), custom_call_target="tpu_custom_call" | custom-call | flops 644874240 | bytes 792588 | tf_op jit(solution)/shard_map/pallas_call | solution.py:270
  (3 shorter events, 0.0 us)
Async XLA Ops:
  0.0 1.9 %copy-start.1 = (f32[4,2,8,256]{3,2,1,0:T(8,128)S(1)}, f32[4,2,8,256]{3,2,1,0:T(8,128)}, u32[]{:S(2)}) copy-start(f32[4,2,8,256]{3,2,1,0:T(8,128)} %param.12) | copy-start | bytes 196612
  0.9 3.0 %collective-permute-start.1 = (bf16[64,256]{1,0:T(8,128)(2,1)S(1)}, bf16[64,256]{1,0:T(8,128)(2,1)S(1)}, u32[]{:S(2)}, u32[]{:S(2)}) collective-permute-start(bf16[64,256]{1,0:T(8,128)(2,1)S(1)} %shard_map.110), channel_id=1, source_target_pairs={{0,1},{1,0},{2,3},{3,2},{4,5},{5,4},{6,7},{7,6},{8,9},{9,8},{10,11... | collective-permute-start | bytes 98312 | tf_op jit(solution)/shard_map/ppermute | solution.py:295
  1.9 0.7 %copy-start.6 = (f32[1,1,256]{2,1,0:T(1,128)S(1)}, f32[1,1,256]{2,1,0:T(1,128)}, u32[]{:S(2)}) copy-start(f32[1,1,256]{2,1,0:T(1,128)} %param.21) | copy-start | bytes 3076
  1.9 0.7 %copy-start.4 = (s32[1,1,256]{2,1,0:T(1,128)S(1)}, s32[1,1,256]{2,1,0:T(1,128)}, u32[]{:S(2)}) copy-start(s32[1,1,256]{2,1,0:T(1,128)} %param.19) | copy-start | bytes 3076
  1.9 0.7 %copy-start.5 = (s32[1,1,256]{2,1,0:T(1,128)S(1)}, s32[1,1,256]{2,1,0:T(1,128)}, u32[]{:S(2)}) copy-start(s32[1,1,256]{2,1,0:T(1,128)} %param.20) | copy-start | bytes 3076
  1.9 0.7 %copy-start.3 = (s32[1,1,256]{2,1,0:T(1,128)S(1)}, s32[1,1,256]{2,1,0:T(1,128)}, u32[]{:S(2)}) copy-start(s32[1,1,256]{2,1,0:T(1,128)} %param.18) | copy-start | bytes 3076
  2.7 5.4 %collective-permute-start = (bf16[48,256]{1,0:T(8,128)(2,1)S(1)}, bf16[48,256]{1,0:T(8,128)(2,1)S(1)}, u32[]{:S(2)}, u32[]{:S(2)}) collective-permute-start(bf16[48,256]{1,0:T(8,128)(2,1)S(1)} %shard_map.109.msg_ref), channel_id=1, source_target_pairs={{0,1},{1,0},{2,3},{3,2},{4,5},{5,4},{6,7},{7,6},{8,9},{9,8},{10,11... | collective-permute-start | bytes 73736 | tf_op jit(solution)/shard_map/ppermute | solution.py:295
  3.9 3.0 %copy-start.9 = (bf16[9,96,18]{1,2,0:T(8,128)(2,1)S(1)}, bf16[9,96,18]{1,2,0:T(8,128)(2,1)}, u32[]{:S(2)}) copy-start(bf16[9,96,18]{1,2,0:T(8,128)(2,1)} %param.14) | copy-start | bytes 93316
  3.9 4.5 %collective-permute-start.2 = (bf16[128,256]{1,0:T(8,128)(2,1)S(1)}, bf16[128,256]{1,0:T(8,128)(2,1)S(1)}, u32[]{:S(2)}, u32[]{:S(2)}) collective-permute-start(bf16[128,256]{1,0:T(8,128)(2,1)S(1)} %pad_maximum_fusion.own_ref), channel_id=1, source_target_pairs={{0,2},{2,0},{4,6},{6,4},{8,10},{10,8},{12,14},{14,12},{16,18},{18,... | collective-permute-start | bytes 196616 | tf_op jit(solution)/shard_map/ppermute | solution.py:304
  5.6 4.6 %collective-permute-start.3 = (bf16[128,256]{1,0:T(8,128)(2,1)S(1)}, bf16[128,256]{1,0:T(8,128)(2,1)S(1)}, u32[]{:S(2)}, u32[]{:S(2)}) collective-permute-start(bf16[128,256]{1,0:T(8,128)(2,1)S(1)} %pad_maximum_fusion.own_ref), channel_id=1, source_target_pairs={{2,4},{4,2},{6,8},{8,6},{10,12},{12,10},{14,16},{16,14},{18,20},{2... | collective-permute-start | bytes 196616 | tf_op jit(solution)/shard_map/ppermute | solution.py:303
  6.9 0.7 %copy-start.2 = (bf16[9,2,96]{2,1,0:T(2,128)(2,1)S(1)}, bf16[9,2,96]{2,1,0:T(2,128)(2,1)}, u32[]{:S(2)}) copy-start(bf16[9,2,96]{2,1,0:T(2,128)(2,1)} %conv_out_ref.1) | copy-start | bytes 10372
  7.1 0.7 %copy-start.7 = (f32[96]{0:T(128)S(1)}, f32[96]{0:T(128)}, u32[]{:S(2)}) copy-start(f32[96]{0:T(128)} %param.16) | copy-start | bytes 1156
  8.1 2.1 %copy-start = (f32[4,2,8,256]{3,2,1,0:T(8,128)S(1)}, f32[4,2,8,256]{3,2,1,0:T(8,128)}, u32[]{:S(2)}) copy-start(f32[4,2,8,256]{3,2,1,0:T(8,128)} %param.11) | copy-start | bytes 196612
  10.2 6.7 %copy-start.8 = (f32[4,2,8,256]{3,2,1,0:T(8,128)S(1)}, f32[4,2,8,256]{3,2,1,0:T(8,128)}, u32[]{:S(2)}) copy-start(f32[4,2,8,256]{3,2,1,0:T(8,128)} %param.13) | copy-start | bytes 196612
  12.4 1.5 %collective-permute-start.4 = (bf16[96,256]{1,0:T(8,128)(2,1)S(1)}, bf16[96,256]{1,0:T(8,128)(2,1)S(1)}, u32[]{:S(2)}, u32[]{:S(2)}) collective-permute-start(bf16[96,256]{1,0:T(8,128)(2,1)S(1)} %get-tuple-element.16.own_ref), channel_id=1, source_target_pairs={{0,2},{2,0},{4,6},{6,4},{8,10},{10,8},{12,14},{14,12},{16,18},{18,... | collective-permute-start | bytes 147464 | tf_op jit(solution)/shard_map/ppermute | solution.py:304
  12.4 4.5 %collective-permute-start.5 = (bf16[96,256]{1,0:T(8,128)(2,1)S(1)}, bf16[96,256]{1,0:T(8,128)(2,1)S(1)}, u32[]{:S(2)}, u32[]{:S(2)}) collective-permute-start(bf16[96,256]{1,0:T(8,128)(2,1)S(1)} %get-tuple-element.16.own_ref), channel_id=1, source_target_pairs={{2,4},{4,2},{6,8},{8,6},{10,12},{12,10},{14,16},{16,14},{18,20},{2... | collective-permute-start | bytes 147464 | tf_op jit(solution)/shard_map/ppermute | solution.py:303

commit v5 on v4

--- a/solution.py
+++ b/solution.py
@@ -15,12 +15,14 @@
 COLS = 256
 HID = 96
 FRAMES = 4
-GROUP = 3 * FL
-BLOCK = 80
-DEPTH = 256
+NEAR = 48
+FAR = 32
+TAPS = 18
+TAP_ROWS = 24
+DEPTH = 3 * (NEAR + FAR)
 AUX_OBS = 4 * FL
 AUX_ROWS = AUX_OBS + 16
-NO_CELL = 64.0
+NO_CELL = 64
 AHEAD, LAG2, LAG3 = 4, 3, 3
 VMEM = pl.BlockSpec(memory_space=pltpu.VMEM)
 SMEM = pl.BlockSpec(memory_space=pltpu.SMEM)
@@ -54,14 +56,15 @@
         msg_ref[row * FL : (row + 2) * FL, :] = pair.astype(BF16)
 
 
-def aux_kernel(count_ref, noise_in, step_ref, row_ref, col_ref, val_ref, aux_ref, noise_ref):
+def aux_kernel(
+    count_ref, noise_in, step_ref, row_ref, col_ref, val_ref, aux_ref, noise_ref
+):
     split_halves(noise_in, noise_ref)
     for at, row in enumerate((0, ROWS - 2)):
         pair = jnp.concatenate([row_of(noise_ref, row), row_of(noise_ref, row + 1)], axis=0)
         aux_ref[2 * at * FL : 2 * (at + 1) * FL, :] = pair.astype(BF16)
     live = iota((1, COLS), 1) < count_ref[...]
-    cell = (row_ref[...] * FL + step_ref[...] * 2).astype(F32)
-    cell = jnp.where(live, cell, NO_CELL)
+    cell = jnp.where(live, row_ref[...] * FL + step_ref[...] * 2, NO_CELL).astype(F32)
     val = val_ref[...]
     high = val.astype(BF16).astype(F32)
     middle = (val - high).astype(BF16).astype(F32)
@@ -73,34 +76,41 @@
     aux_ref[AUX_OBS:AUX_ROWS, :] = table.astype(BF16)
 
 
-def weights_kernel(conv_in_ref, conv_out_ref, embed_ref, w1_ref, w2_ref, wide_ref):
-    halves = [jnp.zeros((HID, 128), F32), jnp.zeros((HID, 128), F32)]
-    wide_ref[...] = jnp.zeros((HID, 128), F32)
+def weights_kernel(flags_ref, taps_ref, conv_out_ref, embed_ref, w1_ref, w2_ref, wide_ref):
+    even, has_far = flags_ref[0] == 1, flags_ref[1] == 1
+    wide_ref[...] = jnp.zeros((9 * TAP_ROWS, HID), F32)
     for at in range(9):
-        wide_ref[:, 0:18] = conv_in_ref[at].astype(F32)
-        start = BLOCK * (at // 3) + GROUP * (at % 3)
-        shifted = wide_ref[...]
-        if start % 128:
-            shifted = pltpu.roll(shifted, start % 128, 1)
-        halves[start // 128] = halves[start // 128] + shifted
+        wide_ref[at * TAP_ROWS : at * TAP_ROWS + TAPS, :] = taps_ref[at].astype(F32)
+    taps = wide_ref[...].astype(BF16)
     square = iota((HID, 128), 0) == iota((HID, 128), 1)
     line = jnp.concatenate([embed_ref[...], jnp.zeros((1, 128 - HID), F32)], axis=1)
     embed = jnp.sum(jnp.where(square, line, 0.0), axis=1, keepdims=True)
     high = embed.astype(BF16).astype(F32)
     middle = (embed - high).astype(BF16).astype(F32)
     low = embed - high - middle
-    lane = iota((HID, 128), 1)
-    bias = jnp.where(lane == 3 * GROUP, high, 0.0)
-    bias = jnp.where(lane == 3 * GROUP + 1, middle, bias)
-    bias = jnp.where(lane == 3 * GROUP + 2, low, bias)
+    lane = iota((HID, DEPTH), 1) - (3 * NEAR + 3 * FL)
+    bias = jnp.where(lane == 0, high, 0.0)
+    bias = jnp.where(lane == 1, middle, bias)
+    bias = jnp.where(lane == 2, low, bias)
+    shape = (TAP_ROWS, DEPTH)
+    lanes = iota(shape, 1)
     for frame in range(FRAMES):
-        left, right = halves
-        if frame:
-            left = pltpu.roll(left, 2 * frame, 1)
-            right = pltpu.roll(right, 2 * frame, 1)
-        rows = slice(frame * HID, (frame + 1) * HID)
-        w1_ref[rows, 0:128] = (0.5 * (left + bias)).astype(BF16)
-        w1_ref[rows, 128:256] = (0.5 * right).astype(BF16)
+        place = iota(shape, 0) + 2 * frame
+        group = place >> 3
+        slot = jnp.where(even, 2 - group, group)
+        within = place & 7
+        parts = []
+        for at in range(9):
+            row_off, col_off = at // 3, at % 3
+            near = row_off * NEAR + col_off * 2 * FL + slot * FL + within
+            far = 3 * NEAR + row_off * FAR + col_off * FL + within
+            target = jnp.where(slot == 2, jnp.where(has_far, far, -1), near)
+            parts.append(jnp.where(lanes == target, 0.5, 0.0))
+        move = jnp.concatenate(parts, axis=0).astype(BF16)
+        out = lax.dot_general(
+            taps, move, (((0,), (0,)), ((), ())), preferred_element_type=F32
+        )
+        w1_ref[frame * HID : (frame + 1) * HID, :] = (out + 0.5 * bias).astype(BF16)
     odd = iota((FL, HID), 0) % 2 == 1
     parts = []
     for at in range(9):
@@ -144,37 +154,46 @@
         total_ref[at : at + cells, :] = total
 
 
-def fill_pair(flags, refs, win_ref, pair, level):
-    even, has_prev, has_next = flags
-    at = slice(2 * pair * FL, 2 * (pair + 1) * FL)
-    core, own, far = (ref[at, :].astype(F32) for ref in refs)
-    prev = jnp.where(has_prev, jnp.where(even, far, core), 0.0)
-    nxt = jnp.where(has_next, jnp.where(even, core, far), 0.0)
+def shifts(here):
+    return [pltpu.roll(here, 1, 1), here, pltpu.roll(here, COLS - 1, 1)]
+
+
+def near_kernel(core_ref, own_ref, near_ref):
+    for pair in range(own_ref.shape[0] // (2 * FL)):
+        at = slice(2 * pair * FL, 2 * (pair + 1) * FL)
+        core, own = core_ref[at, :].astype(F32), own_ref[at, :].astype(F32)
+        for sub in range(2):
+            part = slice(sub * FL, (sub + 1) * FL)
+            here = jnp.concatenate([core[part], own[part]], axis=0)
+            block = jnp.concatenate(shifts(here), axis=0)
+            start = (2 * pair + sub) * NEAR
+            near_ref[start : start + NEAR, :] = block.astype(BF16)
+
+
+def fill_pair(ref, win_ref, pair, level):
+    far = ref[2 * pair * FL : 2 * (pair + 1) * FL, :].astype(F32)
     const = jnp.full((FL, COLS), level, F32)
     for sub in range(2):
-        part = slice(sub * FL, (sub + 1) * FL)
-        here = jnp.concatenate([prev[part], own[part], nxt[part]], axis=0)
-        block = jnp.concatenate(
-            [pltpu.roll(here, 1, 1), here, pltpu.roll(here, COLS - 1, 1), const], axis=0
-        )
-        start = (2 * pair + sub) * BLOCK
-        win_ref[start : start + BLOCK, :] = block.astype(BF16)
-
-
-def run_rows(flags_ref, refs, w1_ref, w2_ref, win_ref, hid_ref, prod_ref, rows, level, emit):
-    flags = [flags_ref[at] == 1 for at in range(3)]
+        here = far[sub * FL : (sub + 1) * FL]
+        block = jnp.concatenate(shifts(here) + [const], axis=0)
+        start = (2 * pair + sub) * FAR
+        win_ref[start : start + FAR, :] = block.astype(BF16)
+
+
+def run_rows(near_ref, far_ref, w1_ref, w2_ref, win_ref, hid_ref, prod_ref, rows, level, emit):
     hidden_rows = rows - 2
     n = FRAMES * HID
-    win_ref[rows * BLOCK : rows * BLOCK + 16, :] = jnp.zeros((16, COLS), BF16)
     filled = 0
     for step in range(hidden_rows + LAG2 + LAG3):
         want = min(rows, step + 3 + AHEAD)
         while 2 * filled < want:
-            fill_pair(flags, refs, win_ref, filled, level)
+            fill_pair(far_ref, win_ref, filled, level)
             filled += 1
         if step < hidden_rows:
-            start = step * BLOCK
-            half = jnp.dot(w1_ref[...], win_ref[start : start + DEPTH, :], preferred_element_type=F32)
+            near = near_ref[step * NEAR : (step + 3) * NEAR, :]
+            far = win_ref[step * FAR : (step + 3) * FAR, :]
+            window = jnp.concatenate([near, far], axis=0)
+            half = jnp.dot(w1_ref[...], window, preferred_element_type=F32)
             hid_ref[step * n : (step + 1) * n, :] = (half + half * jnp.tanh(half)).astype(BF16)
         row = step - LAG2
         if 0 <= row < hidden_rows:
@@ -208,8 +227,8 @@
 
 
 def first_kernel(
-    flags_ref, x_in, noise_in, aux_up_ref, aux_down_ref, core_ref, own_ref, far_ref, w1_ref,
-    w2_ref, count_ref, total_ref, next_ref, send_ref, win_ref, hid_ref, prod_ref, x_ref, noise_ref,
+    x_in, noise_in, aux_up_ref, aux_down_ref, near_ref, own_ref, far_ref, w1_ref, w2_ref,
+    count_ref, total_ref, next_ref, send_ref, win_ref, hid_ref, prod_ref, x_ref, noise_ref,
 ):
     split_halves(x_in, x_ref)
     split_halves(noise_in, noise_ref)
@@ -236,13 +255,12 @@
             send_ref[(here - 1) * FL : (here + 1) * FL, :] = pair.astype(BF16)
 
     run_rows(
-        flags_ref, (core_ref, own_ref, far_ref), w1_ref, w2_ref, win_ref, hid_ref, prod_ref,
-        2 * ROWS, LEVELS[0], emit,
+        near_ref, far_ref, w1_ref, w2_ref, win_ref, hid_ref, prod_ref, 2 * ROWS, LEVELS[0], emit
     )
 
 
 def second_kernel(
-    flags_ref, x_ref, noise_in, core_ref, own_ref, far_ref, w1_ref, w2_ref,
+    x_ref, noise_in, near_ref, far_ref, w1_ref, w2_ref,
     count_ref, total_ref, out_ref, win_ref, hid_ref, prod_ref, noise_ref, half_ref,
 ):
     split_halves(noise_in, noise_ref)
@@ -257,8 +275,7 @@
         half_ref[pl.ds(ROWS * FL + row, FL, stride=ROWS), :] = new[:, 128:256]
 
     run_rows(
-        flags_ref, (core_ref, own_ref, far_ref), w1_ref, w2_ref, win_ref, hid_ref, prod_ref,
-        ROWS + 4, LEVELS[1], emit,
+        near_ref, far_ref, w1_ref, w2_ref, win_ref, hid_ref, prod_ref, ROWS + 4, LEVELS[1], emit
     )
     out_ref[:, 0:128] = half_ref[0 : ROWS * FL, :]
     out_ref[:, 128:256] = half_ref[ROWS * FL :, :]
@@ -308,7 +325,7 @@
 def scratch_for(rows):
     halves = pltpu.VMEM((2 * ROWS * FL, 128), F32)
     return [
-        pltpu.VMEM((rows * BLOCK + 16, COLS), BF16),
+        pltpu.VMEM((rows * FAR, COLS), BF16),
         pltpu.VMEM(((rows - 2) * FRAMES * HID, COLS), BF16),
         pltpu.VMEM(((rows - 2) * 72, COLS), F32),
         halves,
@@ -316,12 +333,20 @@
     ]
 
 
+def near_call(core, own):
+    rows = own.shape[0] // FL
+    (near,) = call(
+        near_kernel, (core, own), [VMEM] * 2, [jax.ShapeDtypeStruct((rows * NEAR, COLS), BF16)]
+    )
+    return near
+
+
 def first_call(*args):
     shape = jax.ShapeDtypeStruct
     return call(
         first_kernel,
         args,
-        [SMEM] + [VMEM] * 11,
+        [VMEM] * 11,
         [shape((ROWS * FL, COLS), F32), shape(((ROWS + 4) * FL, COLS), BF16)],
         scratch_for(2 * ROWS),
         flops=14 * 2 * 256 * 384 * (256 + 72),
@@ -332,7 +357,7 @@
     (out,) = call(
         second_kernel,
         args,
-        [SMEM] + [VMEM] * 9,
+        [VMEM] * 8,
         [jax.ShapeDtypeStruct((FL * ROWS, COLS), F32)],
         scratch_for(ROWS + 4),
         flops=10 * 2 * 256 * 384 * (256 + 72),
@@ -353,14 +378,9 @@
     x, noise_a, noise_b = flat(noisy_states), flat(noise_first), flat(noise_second)
     shape = jax.ShapeDtypeStruct
     here = lax.axis_index("tm")
-    flags = jnp.stack(
-        [
-            (here % 2 == 0).astype(jnp.int32),
-            (here > 0).astype(jnp.int32),
-            (here < n_tm - 1).astype(jnp.int32),
-        ]
-    )
-
+    even = here % 2 == 0
+    has_far = jnp.where(even, here > 0, here < n_tm - 1)
+    flags = jnp.stack([even, has_far]).astype(jnp.int32)
     scaled = (x / (1.0 + LEVELS[0] ** 2) ** 0.5).astype(BF16)
     halves = pltpu.VMEM((2 * ROWS * FL, 128), F32)
     (msg,) = call(pack_kernel, (scaled,), [VMEM], [shape((ROWS * FL, COLS), BF16)], [halves])
@@ -375,21 +395,23 @@
     aux_up, aux_down = exchange_rows(aux, n_rows)
     w1, w2 = call(
         weights_kernel,
-        (conv_in, conv_out, line(level_embed)),
-        [VMEM] * 3,
+        (flags, conv_in.transpose(0, 2, 1), conv_out, line(level_embed)),
+        [SMEM] + [VMEM] * 3,
         [shape((FRAMES * HID, DEPTH), BF16), shape((72, FRAMES * HID), BF16)],
-        [pltpu.VMEM((HID, 128), F32)],
+        [pltpu.VMEM((9 * TAP_ROWS, HID), F32)],
     )
     half = ROWS * FL // 2
     own = jnp.concatenate([up[half:], msg, down[:half]], axis=0)
     core, far = exchange_time(own, n_tm, n_rows)
     maps = shape(((ROWS + 4) * FL, COLS), F32)
     count, total = call(maps_kernel, (aux, aux_up, aux_down), [VMEM] * 3, [maps, maps])
+    near = near_call(core, own)
     current, send = first_call(
-        flags, x, noise_a, aux_up, aux_down, core, own, far, w1, w2, count, total
+        x, noise_a, aux_up, aux_down, near, own, far, w1, w2, count, total
     )
     core, far = exchange_time(send, n_tm, n_rows)
-    out = second_call(flags, current, noise_b, core, send, far, w1, w2, count, total)
+    near = near_call(core, send)
+    out = second_call(current, noise_b, near, far, w1, w2, count, total)
     return out.reshape(noisy_states.shape)
 
 

time: 19.6 us -> 18.9 us (0.964)
  the two profiles are of different devices: /device:TPU:15 before, /device:TPU:0 now
where the time goes in v5:
time: 18.9 us; the launch traced here: 18.7 us
  starting transfers between devices  6.91 us (37%)
  Pallas kernels  4.84 us (26%)
  waiting for transfers between devices  3.19 us (17%)
  local copies, waits for them, and re-layouts  1.99 us (11%)
  other arithmetic  0.96 us (5%)
  between operations  0.81 us (4%)
    pallas_call x8, Pallas kernels, call(): pl.pallas_call(kernel, out_shape=tuple(outs), in_specs=specs, out_specs=t...  4.84 us
    ppermute x2, starting transfers between devices, exchange_time(): far = lax.ppermute(block, ('tm', 'rows'), far_pairs)  3.29 us
    ppermute x2, starting transfers between devices, exchange_rows(): lax.ppermute(block, 'rows', [(i, (i + 1) % n_rows) for i in range(n_rows)])  3.05 us
    ppermute x2, waiting for transfers between devices, exchange_time(): far = lax.ppermute(block, ('tm', 'rows'), far_pairs)  2.8 us
    unnamed x20, local copies, waits for them, and re-layouts  1.99 us
    convert_element_type x1, other arithmetic, per_device(): scaled = (x / (1.0 + LEVELS[0] ** 2) ** 0.5).astype(BF16)  0.88 us
    ppermute x2, starting transfers between devices, exchange_time(): core = lax.ppermute(block, ('tm', 'rows'), core_pairs)  0.58 us
    ppermute x2, waiting for transfers between devices, exchange_rows(): lax.ppermute(block, 'rows', [(i, (i + 1) % n_rows) for i in range(n_rows)])  0.39 us
  transfers between devices with their start and end apart: 6, of which 2 were waited for; matrix products, arithmetic and copies ran while one was open for 0% of the time, Pallas kernels for 8%

profile of v5, /device:TPU:0, one launch (start us, length us, event | category | flops | bytes accessed | tf_op | source)
XLA Modules:
  0.0 18.7 jit_solution(1397529775920329226)
XLA Ops:
  0.0 0.0 copy-start.1
  0.0 0.9 %multiply_convert_fusion.scaled_in = bf16[64,256]{1,0:T(8,128)(2,1)S(1)} fusion(f32[4,2,8,256]{3,2,1,0:T(8,128)} %param.11), kind=kLoop, calls=%fused_computation.1 | loop fusion | flops 32768 | bytes 98304 | tf_op jit(solution)/shard_map/convert_element_type | solution.py:384
  0.9 3.0 %collective-permute-start.1 = (bf16[64,256]{1,0:T(8,128)(2,1)S(1)}, bf16[64,256]{1,0:T(8,128)(2,1)S(1)}, u32[]{:S(2)}, u32[]{:S(2)}) collective-permute-start(bf16[64,256]{1,0:T(8,128)(2,1)S(1)} %shard_map.110), channel_id=1, source_target_pairs={{0,1},{1,0},{2,3},{3,2},{4,5},{5,4},{6,7},{7,6},{8,9},{9,8},{10,11... | collective-permute-start | bytes 98312 | tf_op jit(solution)/shard_map/ppermute | solution.py:312
  4.6 0.0 copy-start.7
  4.6 0.0 copy-start.5
  4.6 0.0 copy-start.6
  4.6 0.0 copy-start.4
  4.6 0.0 copy-done.1
  4.6 0.6 %copy-done.7 = f32[1,1,256]{2,1,0:T(1,128)S(1)} copy-done((f32[1,1,256]{2,1,0:T(1,128)S(1)}, f32[1,1,256]{2,1,0:T(1,128)}, u32[]{:S(2)}) %copy-start.7) | copy-done | bytes 1048
  5.3 0.0 copy-done.5
  5.3 0.0 copy-done.6
  5.3 0.0 copy-done.4
  5.3 0.1 shard_map.109.msg_ref
  5.4 0.0 collective-permute-start
  5.4 0.4 %collective-permute-done.1 = bf16[64,256]{1,0:T(8,128)(2,1)S(1)} collective-permute-done((bf16[64,256]{1,0:T(8,128)(2,1)S(1)}, bf16[64,256]{1,0:T(8,128)(2,1)S(1)}, u32[]{:S(2)}, u32[]{:S(2)}) %collective-permute-start.1) | collective-permute-done | bytes 32800 | tf_op jit(solution)/shard_map/ppermute | solution.py:312
  5.8 0.0 copy-start.2
  5.8 0.0 copy-start.3
  5.9 2.1 %collective-permute-start.3 = (bf16[128,256]{1,0:T(8,128)(2,1)S(1)}, bf16[128,256]{1,0:T(8,128)(2,1)S(1)}, u32[]{:S(2)}, u32[]{:S(2)}) collective-permute-start(bf16[128,256]{1,0:T(8,128)(2,1)S(1)} %pad_maximum_fusion.own_ref), channel_id=1, source_target_pairs={{2,4},{4,2},{6,8},{8,6},{10,12},{12,10},{14,16},{16,14},{18,20},{2... | collective-permute-start | bytes 196616 | tf_op jit(solution)/shard_map/ppermute | solution.py:320
  7.9 0.1 collective-permute-start.2
  8.1 0.1 add_convert_fusion.flags_ref
  8.2 0.0 copy-start.8
  8.2 0.0 copy-done.2
  8.2 0.0 copy-done.3
  8.2 0.6 %copy-done.8 = f32[96]{0:T(128)S(1)} copy-done((f32[96]{0:T(128)S(1)}, f32[96]{0:T(128)}, u32[]{:S(2)}) %copy-start.8) | copy-done | bytes 408
  8.8 0.9 %shard_map.112 = (bf16[384,240]{1,0:T(8,128)(2,1)S(1)}, bf16[72,384]{1,0:T(8,128)(2,1)S(1)}) custom-call(s32[2]{0:T(128)S(1)} %add_convert_fusion.flags_ref, bf16[9,18,96]{2,1,0:T(8,128)(2,1)S(1)} %bitcast.16, bf16[9,2,96]{2,1,0:T(2,128)(2,1)S(1)} %copy-done.3, f32[1,96]{1,0:T(1,128)S(1)} %bitcast.21), custom_call_target="tpu_custom_call" | custom-call | bytes 274568 | tf_op jit(solution)/shard_map/pallas_call | solution.py:287
  9.7 0.0 collective-permute-done.up_ref.down_ref.aux_up_ref.aux_down_ref
  9.7 0.3 %shard_map.113 = (f32[96,256]{1,0:T(8,128)S(1)}, f32[96,256]{1,0:T(8,128)S(1)}) custom-call(bf16[48,256]{1,0:T(8,128)(2,1)S(1)} %shard_map.109.msg_ref, bf16[48,256]{1,0:T(8,128)(2,1)S(1)} %collective-permute-done.up_ref.down_ref.aux_up_ref.aux_down_ref, bf16[48,256]{1,0:T(8,128)(2,1)S(1)} %collective-permute-done.up_ref.down_ref.aux_up_ref.aux_down_ref), custom_call_target="tpu_custom_call" | custom-call | bytes 270336 | tf_op jit(solution)/shard_map/pallas_call | solution.py:287
  10.0 0.0 copy-start
  10.0 0.0 collective-permute-done.2.core_ref
  10.0 0.1 shard_map.111.near_ref
  10.1 0.0 collective-permute-done.3.far_ref
  10.2 0.6 %copy-done = f32[4,2,8,256]{3,2,1,0:T(8,128)S(1)} copy-done((f32[4,2,8,256]{3,2,1,0:T(8,128)S(1)}, f32[4,2,8,256]{3,2,1,0:T(8,128)}, u32[]{:S(2)}) %copy-start) | copy-done | bytes 65560
  10.8 1.5 %shard_map.114 = (f32[64,256]{1,0:T(8,128)S(1)}, bf16[96,256]{1,0:T(8,128)(2,1)S(1)}) custom-call(f32[64,256]{1,0:T(8,128)S(1)} %bitcast.13, f32[64,256]{1,0:T(8,128)S(1)} %bitcast.15, bf16[48,256]{1,0:T(8,128)(2,1)S(1)} %collective-permute-done.up_ref.down_ref.aux_up_ref.aux_down_ref, ...), custom_call_target="tpu_custom_call" | custom-call | flops 902823936 | bytes 1255424 | tf_op jit(solution)/shard_map/pallas_call | solution.py:287
  12.3 0.0 copy-start.9
  12.3 0.4 %collective-permute-start.4 = (bf16[96,256]{1,0:T(8,128)(2,1)S(1)}, bf16[96,256]{1,0:T(8,128)(2,1)S(1)}, u32[]{:S(2)}, u32[]{:S(2)}) collective-permute-start(bf16[96,256]{1,0:T(8,128)(2,1)S(1)} %get-tuple-element.16.own_ref), channel_id=1, source_target_pairs={{0,2},{2,0},{4,6},{6,4},{8,10},{10,8},{12,14},{14,12},{16,18},{18,... | collective-permute-start | bytes 147464 | tf_op jit(solution)/shard_map/ppermute | solution.py:321
  12.8 1.2 %collective-permute-start.5 = (bf16[96,256]{1,0:T(8,128)(2,1)S(1)}, bf16[96,256]{1,0:T(8,128)(2,1)S(1)}, u32[]{:S(2)}, u32[]{:S(2)}) collective-permute-start(bf16[96,256]{1,0:T(8,128)(2,1)S(1)} %get-tuple-element.16.own_ref), channel_id=1, source_target_pairs={{2,4},{4,2},{6,8},{8,6},{10,12},{12,10},{14,16},{16,14},{18,20},{2... | collective-permute-start | bytes 147464 | tf_op jit(solution)/shard_map/ppermute | solution.py:320
  14.0 0.0 collective-permute-done.4.core_ref
  14.0 0.1 shard_map.115.near_ref
  14.1 2.8 %collective-permute-done.5.far_ref = bf16[96,256]{1,0:T(8,128)(2,1)S(1)} collective-permute-done((bf16[96,256]{1,0:T(8,128)(2,1)S(1)}, bf16[96,256]{1,0:T(8,128)(2,1)S(1)}, u32[]{:S(2)}, u32[]{:S(2)}) %collective-permute-start.5) | collective-permute-done | bytes 49184 | tf_op jit(solution)/shard_map/ppermute | solution.py:320
  16.9 0.0 copy-done.9
  16.9 1.8 %shard_map.116 = f32[64,256]{1,0:T(8,128)} custom-call(f32[64,256]{1,0:T(8,128)S(1)} %get-tuple-element.15.x_ref, f32[64,256]{1,0:T(8,128)S(1)} %bitcast.22, bf16[576,256]{1,0:T(8,128)(2,1)S(1)} %shard_map.115.near_ref, bf16[96,256]{1,0:T(8,128)(2,1)S(1)} %collective-permute-done.5.far_ref, bf16[384,240]{1,0:T(8,128)(2,1)S(1)} %get-tuple-element.11.w1_ref, ...), custom_call_target="tpu_custom_call" | custom-call | flops 644874240 | bytes 976896 | tf_op jit(solution)/shard_map/pallas_call | solution.py:287
  (3 shorter events, 0.0 us)
Async XLA Ops:
  0.0 4.6 %copy-start.1 = (f32[4,2,8,256]{3,2,1,0:T(8,128)S(1)}, f32[4,2,8,256]{3,2,1,0:T(8,128)}, u32[]{:S(2)}) copy-start(f32[4,2,8,256]{3,2,1,0:T(8,128)} %param.12) | copy-start | bytes 196612
  0.9 4.9 %collective-permute-start.1 = (bf16[64,256]{1,0:T(8,128)(2,1)S(1)}, bf16[64,256]{1,0:T(8,128)(2,1)S(1)}, u32[]{:S(2)}, u32[]{:S(2)}) collective-permute-start(bf16[64,256]{1,0:T(8,128)(2,1)S(1)} %shard_map.110), channel_id=1, source_target_pairs={{0,1},{1,0},{2,3},{3,2},{4,5},{5,4},{6,7},{7,6},{8,9},{9,8},{10,11... | collective-permute-start | bytes 98312 | tf_op jit(solution)/shard_map/ppermute | solution.py:312
  4.6 0.7 %copy-start.7 = (f32[1,1,256]{2,1,0:T(1,128)S(1)}, f32[1,1,256]{2,1,0:T(1,128)}, u32[]{:S(2)}) copy-start(f32[1,1,256]{2,1,0:T(1,128)} %param.21) | copy-start | bytes 3076
  4.6 0.7 %copy-start.5 = (s32[1,1,256]{2,1,0:T(1,128)S(1)}, s32[1,1,256]{2,1,0:T(1,128)}, u32[]{:S(2)}) copy-start(s32[1,1,256]{2,1,0:T(1,128)} %param.19) | copy-start | bytes 3076
  4.6 0.7 %copy-start.6 = (s32[1,1,256]{2,1,0:T(1,128)S(1)}, s32[1,1,256]{2,1,0:T(1,128)}, u32[]{:S(2)}) copy-start(s32[1,1,256]{2,1,0:T(1,128)} %param.20) | copy-start | bytes 3076
  4.6 0.7 %copy-start.4 = (s32[1,1,256]{2,1,0:T(1,128)S(1)}, s32[1,1,256]{2,1,0:T(1,128)}, u32[]{:S(2)}) copy-start(s32[1,1,256]{2,1,0:T(1,128)} %param.18) | copy-start | bytes 3076
  5.4 4.3 %collective-permute-start = (bf16[48,256]{1,0:T(8,128)(2,1)S(1)}, bf16[48,256]{1,0:T(8,128)(2,1)S(1)}, u32[]{:S(2)}, u32[]{:S(2)}) collective-permute-start(bf16[48,256]{1,0:T(8,128)(2,1)S(1)} %shard_map.109.msg_ref), channel_id=1, source_target_pairs={{0,1},{1,0},{2,3},{3,2},{4,5},{5,4},{6,7},{7,6},{8,9},{9,8},{10,11... | collective-permute-start | bytes 73736 | tf_op jit(solution)/shard_map/ppermute | solution.py:312
  5.8 2.3 %copy-start.2 = (bf16[9,96,18]{1,2,0:T(8,128)(2,1)S(1)}, bf16[9,96,18]{1,2,0:T(8,128)(2,1)}, u32[]{:S(2)}) copy-start(bf16[9,96,18]{1,2,0:T(8,128)(2,1)} %param.14) | copy-start | bytes 93316
  5.8 2.3 %copy-start.3 = (bf16[9,2,96]{2,1,0:T(2,128)(2,1)S(1)}, bf16[9,2,96]{2,1,0:T(2,128)(2,1)}, u32[]{:S(2)}) copy-start(bf16[9,2,96]{2,1,0:T(2,128)(2,1)} %conv_out_ref.1) | copy-start | bytes 10372
  5.9 4.3 %collective-permute-start.3 = (bf16[128,256]{1,0:T(8,128)(2,1)S(1)}, bf16[128,256]{1,0:T(8,128)(2,1)S(1)}, u32[]{:S(2)}, u32[]{:S(2)}) collective-permute-start(bf16[128,256]{1,0:T(8,128)(2,1)S(1)} %pad_maximum_fusion.own_ref), channel_id=1, source_target_pairs={{2,4},{4,2},{6,8},{8,6},{10,12},{12,10},{14,16},{16,14},{18,20},{2... | collective-permute-start | bytes 196616 | tf_op jit(solution)/shard_map/ppermute | solution.py:320
  7.9 2.0 %collective-permute-start.2 = (bf16[128,256]{1,0:T(8,128)(2,1)S(1)}, bf16[128,256]{1,0:T(8,128)(2,1)S(1)}, u32[]{:S(2)}, u32[]{:S(2)}) collective-permute-start(bf16[128,256]{1,0:T(8,128)(2,1)S(1)} %pad_maximum_fusion.own_ref), channel_id=1, source_target_pairs={{0,2},{2,0},{4,6},{6,4},{8,10},{10,8},{12,14},{14,12},{16,18},{18,... | collective-permute-start | bytes 196616 | tf_op jit(solution)/shard_map/ppermute | solution.py:321
  8.2 0.7 %copy-start.8 = (f32[96]{0:T(128)S(1)}, f32[96]{0:T(128)}, u32[]{:S(2)}) copy-start(f32[96]{0:T(128)} %param.16) | copy-start | bytes 1156
  10.0 0.8 %copy-start = (f32[4,2,8,256]{3,2,1,0:T(8,128)S(1)}, f32[4,2,8,256]{3,2,1,0:T(8,128)}, u32[]{:S(2)}) copy-start(f32[4,2,8,256]{3,2,1,0:T(8,128)} %param.11) | copy-start | bytes 196612
  12.3 4.5 %copy-start.9 = (f32[4,2,8,256]{3,2,1,0:T(8,128)S(1)}, f32[4,2,8,256]{3,2,1,0:T(8,128)}, u32[]{:S(2)}) copy-start(f32[4,2,8,256]{3,2,1,0:T(8,128)} %param.13) | copy-start | bytes 196612
  12.3 1.6 %collective-permute-start.4 = (bf16[96,256]{1,0:T(8,128)(2,1)S(1)}, bf16[96,256]{1,0:T(8,128)(2,1)S(1)}, u32[]{:S(2)}, u32[]{:S(2)}) collective-permute-start(bf16[96,256]{1,0:T(8,128)(2,1)S(1)} %get-tuple-element.16.own_ref), channel_id=1, source_target_pairs={{0,2},{2,0},{4,6},{6,4},{8,10},{10,8},{12,14},{14,12},{16,18},{18,... | collective-permute-start | bytes 147464 | tf_op jit(solution)/shard_map/ppermute | solution.py:321
  12.8 4.1 %collective-permute-start.5 = (bf16[96,256]{1,0:T(8,128)(2,1)S(1)}, bf16[96,256]{1,0:T(8,128)(2,1)S(1)}, u32[]{:S(2)}, u32[]{:S(2)}) collective-permute-start(bf16[96,256]{1,0:T(8,128)(2,1)S(1)} %get-tuple-element.16.own_ref), channel_id=1, source_target_pairs={{2,4},{4,2},{6,8},{8,6},{10,12},{12,10},{14,16},{16,14},{18,20},{2... | collective-permute-start | bytes 147464 | tf_op jit(solution)/shard_map/ppermute | solution.py:320
